TPU v7x, 32 devices: a whole 2x2x4 slice. The times are simulated.
32 devices in a mesh: rep: 4 (over x, core), shard: 8 (over z, y).
Axes of the slice: x: 2, y: 2, z: 4, core: 2. Of those that a mesh axis runs over, the one named last changes fastest.
Arguments:
- layer_input: bfloat16 [32, 1024, 768], P(('rep', 'shard')), may hold values from -6 to 6
- in_weight: bfloat16 [768, 2304], P('shard'), may hold values from -0.21875 to 0.21875
- query_bias: bfloat16 [768], P('shard'), may hold values from -4 to 4
- value_bias: bfloat16 [768], P('shard'), may hold values from -1.5 to 1.5
- out_weight: bfloat16 [768, 768], P('shard'), may hold values from -0.875 to 0.875
- out_bias: bfloat16 [768], P('shard'), may hold values from -3 to 3
- first_gain: bfloat16 [768], P('shard'), may hold values from 0.5 to 1.5
- first_shift: bfloat16 [768], P('shard'), may hold values from -3 to 3
- inner_weight: bfloat16 [768, 3072], P('shard'), may hold values from -0.21875 to 0.21875
- inner_bias: bfloat16 [3072], P('shard'), may hold values from -4 to 4
- outer_weight: bfloat16 [3072, 768], P('shard'), may hold values from -0.15625 to 0.15625
- outer_bias: bfloat16 [768], P('shard'), may hold values from -3 to 3
- second_gain: bfloat16 [768], P('shard'), may hold values from 0.5 to 1.5
- second_shift: bfloat16 [768], P('shard'), may hold values from -3 to 3
- segment_ids: int32 [32, 1024], P(('rep', 'shard')), may hold values from 0 to 3, never falling along the last dimension, each value on 1 to 512 neighbouring positions
- token_valid: int32 [32, 1024], P(('rep', 'shard')), may hold values from 0 to 1, as said below
- query_perm: int32 [32, 12, 1024], P(('rep', 'shard')), may hold values from 0 to 1023, each once within a row
- key_perm: int32 [32, 12, 1024], P(('rep', 'shard')), may hold values from 0 to 1023, each once within a row
- out_cotangent: bfloat16 [32, 1024, 768], P(('rep', 'shard')), may hold values from -6 to 6
Outputs:
- hidden_out: bfloat16 [32, 1024, 768], P(('rep', 'shard'))
- input_grad: bfloat16 [32, 1024, 768], P(('rep', 'shard'))
- grad_in_weight: float32 [768, 2304], P('shard')
- grad_query_bias: float32 [768], P('shard')
- grad_value_bias: float32 [768], P('shard')
- grad_out_weight: float32 [768, 768], P('shard')
- grad_out_bias: float32 [768], P('shard')
- grad_first_gain: float32 [768], P('shard')
- grad_first_shift: float32 [768], P('shard')
- grad_inner_weight: float32 [768, 3072], P('shard')
- grad_inner_bias: float32 [3072], P('shard')
- grad_outer_weight: float32 [3072, 768], P('shard')
- grad_outer_bias: float32 [768], P('shard')
- grad_second_gain: float32 [768], P('shard')
- grad_second_shift: float32 [768], P('shard')
Inputs may be any that keep to these rules, and one draw needn't show every extreme that they name: `token_valid`: in each sequence the real tokens come first and at least one last position is padding (0), at most 128 positions. `segment_ids`: numbers never fall along a sequence. `query_perm`: for each sequence and head, a permutation of the positions. `key_perm`: for each sequence and head, a permutation of the positions.
All inputs are finite; a program needn't handle non-finite values.
Results may differ from a plain program's by a relative error of at most 0.015.
Values may be sent and summed in bfloat16 or wider, within the bound.
A program may use at most 256 MiB of HBM per device.

v0:
```python
from functools import partial

import jax
import jax.numpy as jnp
from jax import lax
from jax.sharding import PartitionSpec as P

CL = 128


EPS = 1e-06


def norm_parts(resid):
    average = jnp.mean(resid, axis=-1, keepdims=True)
    centred = resid - average
    variance = jnp.mean(centred * centred, axis=-1, keepdims=True)
    inv_std = lax.rsqrt(variance + EPS)
    return (centred * inv_std, inv_std)


def norm_back(grad_out, normed, inv_std, gain):
    scaled = grad_out * gain
    first_term = jnp.mean(scaled, axis=-1, keepdims=True)
    second_term = jnp.mean(scaled * normed, axis=-1, keepdims=True)
    grad_in = inv_std * (scaled - first_term - normed * second_term)
    return (grad_in, jnp.sum(grad_out * normed, axis=0), jnp.sum(grad_out, axis=0))


def invert_order(order):

    def single(row_order):
        return (
            jnp.zeros_like(row_order)
            .at[row_order]
            .set(jnp.arange(row_order.shape[0], dtype=jnp.int32))
        )

    return jax.vmap(jax.vmap(single))(order)


def to_heads(tensor, seqs, heads):
    tokens, width = tensor.shape
    return jnp.transpose(tensor.reshape(seqs, tokens // seqs, heads, width // heads), (0, 2, 1, 3))


def from_heads(tensor):
    seqs, heads, length, head_size = tensor.shape
    return jnp.transpose(tensor, (0, 2, 1, 3)).reshape(seqs * length, heads * head_size)


def arrange(tensor, order):
    return jnp.take_along_axis(tensor, order[..., None], axis=2)


def in_clusters(tensor):
    seqs, heads, length, inner_dim = tensor.shape
    return tensor.reshape(seqs, heads, length // CL, CL, inner_dim)


def shards(
    layer_input,
    in_weight,
    query_bias,
    value_bias,
    out_weight,
    out_bias,
    first_gain,
    first_shift,
    inner_weight,
    inner_bias,
    outer_weight,
    outer_bias,
    second_gain,
    second_shift,
    segment_ids,
    token_valid,
    query_perm,
    key_perm,
    out_cotangent,
):
    seqs, length, width = layer_input.shape
    heads = query_perm.shape[1]
    head_size = width // heads
    scale = head_size ** (-0.5)
    tokens = seqs * length
    gathered = (
        lax.all_gather(in_weight, "shard", axis=0, tiled=True),
        lax.all_gather(query_bias, "shard", axis=0, tiled=True),
        lax.all_gather(value_bias, "shard", axis=0, tiled=True),
        lax.all_gather(out_weight, "shard", axis=0, tiled=True),
        lax.all_gather(out_bias, "shard", axis=0, tiled=True),
        lax.all_gather(first_gain, "shard", axis=0, tiled=True),
        lax.all_gather(first_shift, "shard", axis=0, tiled=True),
        lax.all_gather(inner_weight, "shard", axis=0, tiled=True),
        lax.all_gather(inner_bias, "shard", axis=0, tiled=True),
        lax.all_gather(outer_weight, "shard", axis=0, tiled=True),
        lax.all_gather(outer_bias, "shard", axis=0, tiled=True),
        lax.all_gather(second_gain, "shard", axis=0, tiled=True),
        lax.all_gather(second_shift, "shard", axis=0, tiled=True),
    )
    (
        w_in,
        b_query,
        b_value,
        w_out,
        b_out,
        g_first,
        s_first,
        w_inner,
        b_inner,
        w_outer,
        b_outer,
        g_second,
        s_second,
    ) = gathered
    flat_in = layer_input.reshape(tokens, width)
    projected = jnp.dot(flat_in, w_in, preferred_element_type=jnp.float32)
    query = (projected[:, :width] + b_query.astype(jnp.float32)).astype(jnp.bfloat16)
    keys = projected[:, width : 2 * width].astype(jnp.bfloat16)
    values = (projected[:, 2 * width :] + b_value.astype(jnp.float32)).astype(jnp.bfloat16)
    q_cl = in_clusters(arrange(to_heads(query, seqs, heads), query_perm))
    k_cl = in_clusters(arrange(to_heads(keys, seqs, heads), key_perm))
    v_cl = in_clusters(arrange(to_heads(values, seqs, heads), key_perm))
    seg_heads = jnp.broadcast_to(segment_ids[:, None, :], query_perm.shape)
    ok_heads = jnp.broadcast_to(token_valid[:, None, :], query_perm.shape)
    cshape = (seqs, heads, length // CL, CL)
    seg_query = jnp.take_along_axis(seg_heads, query_perm, axis=2).reshape(cshape)
    seg_key = jnp.take_along_axis(seg_heads, key_perm, axis=2).reshape(cshape)
    ok_query = jnp.take_along_axis(ok_heads, query_perm, axis=2).reshape(cshape)
    ok_key = jnp.take_along_axis(ok_heads, key_perm, axis=2).reshape(cshape)
    visible = (
        (seg_query[..., :, None] == seg_key[..., None, :])
        & (ok_query[..., :, None] > 0)
        & (ok_key[..., None, :] > 0)
    )
    scores = (
        jnp.einsum("shcie,shcje->shcij", q_cl, k_cl, preferred_element_type=jnp.float32) * scale
    )
    maxima = jnp.max(jnp.where(visible, scores, -1e30), axis=-1, keepdims=True)
    raised = jnp.where(visible, jnp.exp(jnp.where(visible, scores - maxima, 0.0)), 0.0)
    divisor = jnp.maximum(jnp.sum(raised, axis=-1, keepdims=True), 1.0)
    probs_low = (raised / divisor).astype(jnp.bfloat16)
    log_total = maxima + jnp.log(divisor)
    combined = jnp.einsum("shcij,shcje->shcie", probs_low, v_cl, preferred_element_type=jnp.float32)
    query_back = invert_order(query_perm)
    key_back = invert_order(key_perm)
    attended = from_heads(
        arrange(combined.reshape(seqs, heads, length, head_size), query_back)
    ).astype(jnp.bfloat16)
    branch = jnp.dot(attended, w_out, preferred_element_type=jnp.float32) + b_out.astype(
        jnp.float32
    )
    first_sum = flat_in.astype(jnp.float32) + branch
    normed_first, inv_first = norm_parts(first_sum)
    first_out = normed_first * g_first.astype(jnp.float32) + s_first.astype(jnp.float32)
    first_low = first_out.astype(jnp.bfloat16)
    inner = jnp.dot(first_low, w_inner, preferred_element_type=jnp.float32) + b_inner.astype(
        jnp.float32
    )
    activated = jax.nn.gelu(inner, approximate=False).astype(jnp.bfloat16)
    outer = jnp.dot(activated, w_outer, preferred_element_type=jnp.float32) + b_outer.astype(
        jnp.float32
    )
    normed_second, inv_second = norm_parts(first_out + outer)
    hidden_out = (
        (normed_second * g_second.astype(jnp.float32) + s_second.astype(jnp.float32))
        .astype(jnp.bfloat16)
        .reshape(seqs, length, width)
    )
    back_in, back_out, back_inner, back_outer, back_gfirst, back_gsecond = (
        w_in,
        w_out,
        w_inner,
        w_outer,
        g_first,
        g_second,
    )
    grad_top = out_cotangent.reshape(tokens, width).astype(jnp.float32)
    d_second, grad_g_second, grad_s_second = norm_back(
        grad_top, normed_second, inv_second, back_gsecond.astype(jnp.float32)
    )
    d_outer = d_second.astype(jnp.bfloat16)
    grad_b_outer = jnp.sum(d_outer, axis=0, dtype=jnp.float32)
    d_activated = jnp.einsum("td,fd->tf", d_outer, back_outer, preferred_element_type=jnp.float32)
    unused, gelu_pull = jax.vjp(partial(jax.nn.gelu, approximate=False), inner)
    d_inner = gelu_pull(d_activated)[0].astype(jnp.bfloat16)
    grad_b_inner = jnp.sum(d_inner, axis=0, dtype=jnp.float32)
    d_first_out = d_second + jnp.einsum(
        "tf,df->td", d_inner, back_inner, preferred_element_type=jnp.float32
    )
    d_first, grad_g_first, grad_s_first = norm_back(
        d_first_out, normed_first, inv_first, back_gfirst.astype(jnp.float32)
    )
    d_branch = d_first.astype(jnp.bfloat16)
    grad_b_out = jnp.sum(d_branch, axis=0, dtype=jnp.float32)
    d_attended = jnp.einsum(
        "te,de->td", d_branch, back_out, preferred_element_type=jnp.float32
    ).astype(jnp.bfloat16)
    do_cl = in_clusters(arrange(to_heads(d_attended, seqs, heads), query_perm))
    again_scores = (
        jnp.einsum("shcie,shcje->shcij", q_cl, k_cl, preferred_element_type=jnp.float32) * scale
    )
    probs = jnp.where(visible, jnp.exp(jnp.where(visible, again_scores - log_total, 0.0)), 0.0)
    d_probs = jnp.einsum("shcie,shcje->shcij", do_cl, v_cl, preferred_element_type=jnp.float32)
    row_terms = jnp.sum(probs * d_probs, axis=-1, keepdims=True)
    d_scores = (probs * (d_probs - row_terms)).astype(jnp.bfloat16)
    dq_cl = (
        jnp.einsum("shcij,shcje->shcie", d_scores, k_cl, preferred_element_type=jnp.float32) * scale
    )
    dk_cl = (
        jnp.einsum("shcij,shcie->shcje", d_scores, q_cl, preferred_element_type=jnp.float32) * scale
    )
    dv_cl = jnp.einsum(
        "shcij,shcie->shcje", probs.astype(jnp.bfloat16), do_cl, preferred_element_type=jnp.float32
    )

    def restore(clustered, back_order):
        return from_heads(arrange(clustered.reshape(seqs, heads, length, head_size), back_order))

    d_proj = jnp.concatenate(
        [restore(dq_cl, query_back), restore(dk_cl, key_back), restore(dv_cl, key_back)], axis=1
    ).astype(jnp.bfloat16)
    grad_b_query = jnp.sum(d_proj[:, :width], axis=0, dtype=jnp.float32)
    grad_b_value = jnp.sum(d_proj[:, 2 * width :], axis=0, dtype=jnp.float32)
    input_grad = (
        (d_first + jnp.einsum("te,de->td", d_proj, back_in, preferred_element_type=jnp.float32))
        .astype(jnp.bfloat16)
        .reshape(seqs, length, width)
    )
    local_shapes = [
        in_weight.shape,
        query_bias.shape,
        value_bias.shape,
        out_weight.shape,
        out_bias.shape,
        first_gain.shape,
        first_shift.shape,
        inner_weight.shape,
        inner_bias.shape,
        outer_weight.shape,
        outer_bias.shape,
        second_gain.shape,
        second_shift.shape,
    ]

    def product_rows(left, right):
        return jnp.einsum("tk,te->ke", left, right, preferred_element_type=jnp.float32).reshape(
            lax.axis_size("shard") * 1, -1
        )

    def vector_rows(vector):
        return vector.reshape(lax.axis_size("shard") * 1, -1)

    pieces = [
        product_rows(flat_in, d_proj),
        vector_rows(grad_b_query),
        vector_rows(grad_b_value),
        product_rows(attended, d_branch),
        vector_rows(grad_b_out),
        vector_rows(grad_g_first),
        vector_rows(grad_s_first),
        product_rows(first_low, d_inner),
        vector_rows(grad_b_inner),
        product_rows(activated, d_outer),
        vector_rows(grad_b_outer),
        vector_rows(grad_g_second),
        vector_rows(grad_s_second),
    ]
    my_rows = lax.psum_scatter(
        jnp.concatenate(pieces, axis=1), "shard", scatter_dimension=0, tiled=True
    )
    my_rows = lax.psum(my_rows.astype(jnp.bfloat16), "rep").astype(jnp.float32)
    flat_mine = my_rows.reshape(-1)
    results = []
    offset = 0
    for shape_here in local_shapes:
        count_here = 1
        for extent_here in shape_here:
            count_here = count_here * extent_here
        results.append(flat_mine[offset : offset + count_here].reshape(shape_here))
        offset = offset + count_here
    return (
        hidden_out,
        input_grad,
        results[0],
        results[1],
        results[2],
        results[3],
        results[4],
        results[5],
        results[6],
        results[7],
        results[8],
        results[9],
        results[10],
        results[11],
        results[12],
    )


def solution(mesh):
    return jax.shard_map(
        shards,
        mesh=mesh,
        in_specs=(
            P(("rep", "shard"), None, None),
            P("shard", None),
            P("shard"),
            P("shard"),
            P("shard", None),
            P("shard"),
            P("shard"),
            P("shard"),
            P("shard", None),
            P("shard"),
            P("shard", None),
            P("shard"),
            P("shard"),
            P("shard"),
            P(("rep", "shard"), None),
            P(("rep", "shard"), None),
            P(("rep", "shard"), None, None),
            P(("rep", "shard"), None, None),
            P(("rep", "shard"), None, None),
        ),
        out_specs=(
            P(("rep", "shard"), None, None),
            P(("rep", "shard"), None, None),
            P("shard", None),
            P("shard"),
            P("shard"),
            P("shard", None),
            P("shard"),
            P("shard"),
            P("shard"),
            P("shard", None),
            P("shard"),
            P("shard", None),
            P("shard"),
            P("shard"),
            P("shard"),
        ),
        check_vma=False,
    )
```

profile of v0, /device:TPU:0, one launch (start us, length us, event | category | flops | bytes accessed | tf_op | source)
XLA Modules:
  0.0 3090.1 jit_solution(8853044434371541928)
XLA Ops:
  13.8 97.2 %gather_fusion.2 = s32[12288]{0:T(1024)S(1)} fusion(s32[12,1024]{1,0:T(8,128)S(1)} %broadcast.664, s32[12288]{0:T(1024)S(1)} %bitcast.233), kind=kCustom, calls=%fused_computation.4.clone | custom fusion | bytes 196608 | tf_op jit(solution)/shard_map/jit(take_along_axis)/gather | solution.py:130
  111.1 97.2 %gather_fusion = s32[12288]{0:T(1024)S(1)} fusion(s32[12,1024]{1,0:T(8,128)S(1)} %broadcast.662, s32[12288]{0:T(1024)S(1)} %bitcast.234), kind=kCustom, calls=%fused_computation.clone | custom fusion | bytes 196608 | tf_op jit(solution)/shard_map/jit(take_along_axis)/gather | solution.py:128
  208.4 97.2 %gather_fusion.3 = s32[12288]{0:T(1024)S(1)} fusion(s32[12,1024]{1,0:T(8,128)S(1)} %broadcast.664, s32[12288]{0:T(1024)S(1)} %bitcast.235), kind=kCustom, calls=%fused_computation.5.clone | custom fusion | bytes 196608 | tf_op jit(solution)/shard_map/jit(take_along_axis)/gather | solution.py:131
  305.8 97.2 %gather_fusion.1 = s32[12288]{0:T(1024)S(1)} fusion(s32[12,1024]{1,0:T(8,128)S(1)} %broadcast.662, s32[12288]{0:T(1024)S(1)} %bitcast.236), kind=kCustom, calls=%fused_computation.3.clone | custom fusion | bytes 196608 | tf_op jit(solution)/shard_map/jit(take_along_axis)/gather | solution.py:129
  404.7 45.4 %scatter_custom_fusion.1 = s32[12288]{0:T(1024)S(1)} fusion(s32[12288]{0:T(1024)S(1)} %reshape.572, s32[12288]{0:T(1024)S(1)} %reshape.566, s32[]{:T(128)} %constant.12.clone.1), kind=kCustom, calls=%fused_computation.151 | custom fusion | bytes 49156
  450.9 45.4 %scatter_custom_fusion = s32[12288]{0:T(1024)S(1)} fusion(s32[12288]{0:T(1024)S(1)} %reshape.564, s32[12288]{0:T(1024)S(1)} %reshape.566, s32[]{:T(128)} %constant.12.clone.1), kind=kCustom, calls=%fused_computation.153 | custom fusion | bytes 49156
  499.6 38.8 %all-reduce.9 = (bf16[768]{0:T(1024)(128)(2,1)S(1)}, bf16[768]{0:T(1024)(128)(2,1)S(1)}, bf16[768]{0:T(1024)(128)(2,1)S(1)}, bf16[768]{0:T(1024)(128)(2,1)S(1)},...) all-reduce(bf16[768]{0:T(1024)(128)(2,1)S(1)} %dynamic-update-slice, ...), channel_id=1, replica_groups=mesh['rep'=4,'shard'=8] {'shard'}, use_global_device_ids=true, to_apply=%add | all-reduce | flops 6144 | bytes 24576
  540.2 25.9 all-gather
  586.3 119.4 %gather_fusion.5 = bf16[12288,64]{1,0:T(8,128)(2,1)} fusion(bf16[12,1024,64]{2,1,0:T(8,128)(2,1)S(1)} %bitcast.237, s32[12288]{0:T(1024)S(1)} %bitcast.231), kind=kCustom, calls=%fused_computation.6.clone | custom fusion | bytes 3244032 | tf_op jit(solution)/shard_map/jit(take_along_axis)/gather | solution.py:53
  713.0 119.4 %gather_fusion.6 = bf16[12288,64]{1,0:T(8,128)(2,1)} fusion(bf16[12,1024,64]{2,1,0:T(8,128)(2,1)S(1)} %bitcast.238, s32[12288]{0:T(1024)S(1)} %bitcast.232), kind=kCustom, calls=%fused_computation.7.clone | custom fusion | bytes 3244032 | tf_op jit(solution)/shard_map/jit(take_along_axis)/gather | solution.py:53
  844.0 119.4 %gather_fusion.4 = bf16[12288,64]{1,0:T(8,128)(2,1)} fusion(bf16[12,1024,64]{2,1,0:T(8,128)(2,1)S(1)} %bitcast.239, s32[12288]{0:T(1024)S(1)} %bitcast.229), kind=kCustom, calls=%fused_computation.1.clone | custom fusion | bytes 3244032 | tf_op jit(solution)/shard_map/jit(take_along_axis)/gather | solution.py:53
  967.2 12.3 select_reduce_fusion
  993.4 119.5 %gather_fusion.7 = bf16[12288,64]{1,0:T(8,128)(2,1)} fusion(bf16[12,1024,64]{2,1,0:T(8,128)(2,1)S(1)} %bitcast.244, s32[12288]{0:T(1024)S(1)} %reshape.741), kind=kCustom, calls=%fused_computation.2.clone | custom fusion | bytes 3244032 | tf_op jit(solution)/shard_map/jit(take_along_axis)/gather | solution.py:53
  1122.0 38.7 %multiply_convert_fusion = (bf16[1024,3072]{1,0:T(8,128)(2,1)}, f32[1024,3072]{1,0:T(8,128)}, f32[1024,3072]{1,0:T(8,128)}) fusion(f32[3072]{0:T(1024)S(1)} %bitcast.302, bf16[768,3072]{1,0:T(8,128)(2,1)} %all-gather.10.cloned.1.call-done, f32[1024,768]{0,1:T(8,128)S(1)} %get-tuple-element.122, f32[768]{0:T(1024)S(1)} %convert_element_type.123, ...), kind=kOutput, calls=%fused_computation.18 | convolution fusion | flops 5043388416 | bytes 39348224 | tf_op jit(solution)/shard_map/dot_general | solution.py:158
  1160.7 9.8 fusion.64
  1182.4 17.4 convert_reduce_fusion
  1199.9 10.6 fusion.56
  1210.5 9.0 multiply_reduce_fusion.1
  1229.4 119.4 %gather_fusion.8 = bf16[12288,64]{1,0:T(8,128)(2,1)} fusion(bf16[12,1024,64]{2,1,0:T(8,128)(2,1)S(1)} %bitcast.240, s32[12288]{0:T(1024)S(1)} %bitcast.230), kind=kCustom, calls=%fused_computation.8.clone | custom fusion | bytes 3244032 | tf_op jit(solution)/shard_map/jit(take_along_axis)/gather | solution.py:53
  1360.9 12.2 multiply_reduce_fusion
  1384.1 9.0 reshape.425
  1399.2 120.2 %gather_fusion.11 = bf16[12288,64]{1,0:T(8,128)(2,1)} fusion(bf16[12,1024,64]{2,1,0:T(8,128)(2,1)S(1)} %bitcast.243, s32[12288]{0:T(1024)S(1)} %copy-done.4), kind=kCustom, calls=%fused_computation.11.clone | custom fusion | bytes 3244032 | tf_op jit(solution)/shard_map/jit(take_along_axis)/gather | solution.py:53
  1523.9 9.0 reshape.427
  1536.0 120.3 %gather_fusion.9 = bf16[12288,64]{1,0:T(8,128)(2,1)} fusion(bf16[12,1024,64]{2,1,0:T(8,128)(2,1)S(1)} %bitcast.241, s32[12288]{0:T(1024)S(1)} %copy-done.6), kind=kCustom, calls=%fused_computation.9.clone | custom fusion | bytes 3244032 | tf_op jit(solution)/shard_map/jit(take_along_axis)/gather | solution.py:53
  1664.5 120.3 %gather_fusion.10 = bf16[12288,64]{1,0:T(8,128)(2,1)} fusion(bf16[12,1024,64]{2,1,0:T(8,128)(2,1)S(1)} %bitcast.242, s32[12288]{0:T(1024)S(1)} %copy-done.4), kind=kCustom, calls=%fused_computation.10.clone | custom fusion | bytes 3244032 | tf_op jit(solution)/shard_map/jit(take_along_axis)/gather | solution.py:53
  1837.9 26.4 dynamic-update-slice.15
  1865.8 26.0 dynamic-update-slice.17
  1896.0 1069.1 %all-reduce.14 = bf16[8,885888]{1,0:T(8,128)(2,1)} all-reduce(f32[8,885888]{1,0:T(8,128)} %dynamic-update-slice.20), channel_id=2, replica_groups=mesh['rep'=4,'shard'=8] {'shard'}, use_global_device_ids=true, to_apply=%region_22.26.clone | all-reduce | flops 7087104 | bytes 42522624
  2965.1 9.1 dynamic-slice_convert_fusion
  2985.3 63.7 %all-reduce.13.cloned.1.call-done = bf16[1,885888]{1,0:T(2,128)(2,1)} async-done(((bf16[1,885888]{1,0:T(2,128)(2,1)}), bf16[1,885888]{1,0:T(2,128)(2,1)}) %all-reduce.13.cloned.1.call-update) | async-done | bytes 1771792 | tf_op jit(solution)/shard_map/psum | solution.py:273
  3057.3 9.1 slice_reduce_fusion.2
  3066.5 12.7 slice_reduce_fusion
  (308 shorter events, 227.7 us)
Async XLA Ops:
  7.2 565.1 %all-gather.6.cloned.1.call-start = ((), (), s32[]{:S(2)}) async-start(), calls=%async_computation | async-start | bytes 3981312 | tf_op jit(solution)/shard_map/all_gather | solution.py:88
  7.9 1109.7 %all-gather.8.cloned.1.call-start = ((), (), s32[]{:S(2)}) async-start(), calls=%async_computation.1 | async-start | bytes 1327104 | tf_op jit(solution)/shard_map/all_gather | solution.py:91
  8.7 1113.3 %all-gather.10.cloned.1.call-start = ((), (), s32[]{:S(2)}) async-start(), calls=%async_computation.2 | async-start | bytes 5308416 | tf_op jit(solution)/shard_map/all_gather | solution.py:95
  9.4 1151.3 %all-gather.12.cloned.1.call-start = ((), (), s32[]{:S(2)}) async-start(), calls=%async_computation.3 | async-start | bytes 5308416 | tf_op jit(solution)/shard_map/all_gather | solution.py:97
  10.0 3039.0 %all-reduce.13.cloned.1.call-start = ((), (), s32[]{:S(2)}) async-start(), calls=%async_computation.4 | async-start | bytes 7087104 | tf_op jit(solution)/shard_map/psum | solution.py:273
  11.9 832.0 %copy-start.2 = (s32[12,1024,1]{1,2,0:T(1,128)}, s32[12,1024,1]{1,2,0:T(1,128)S(1)}, u32[]{:S(2)}) copy-start(s32[12,1024,1]{1,2,0:T(1,128)S(1)} %get-tuple-element.110) | copy-start | bytes 147460
  13.8 97.3 %copy-start.49 = (s32[1,1024]{1,0:T(1,128)S(1)}, s32[1,1024]{1,0:T(1,128)}, u32[]{:S(2)}) copy-start(s32[1,1024]{1,0:T(1,128)} %param.39) | copy-start | bytes 12292
  305.6 97.5 %copy-start.30 = (s32[1,12,1024]{2,0,1:T(1,128)S(1)}, s32[1,12,1024]{2,0,1:T(1,128)}, u32[]{:S(2)}) copy-start(s32[1,12,1024]{2,0,1:T(1,128)} %param.41) | copy-start | bytes 147460
  305.6 97.6 %copy-start.31 = (s32[1,12,1024]{2,0,1:T(1,128)S(1)}, s32[1,12,1024]{2,0,1:T(1,128)}, u32[]{:S(2)}) copy-start(s32[1,12,1024]{2,0,1:T(1,128)} %param.42) | copy-start | bytes 147460
  305.6 97.8 %copy-start.54 = (s32[3]{0:T(128)S(1)}, s32[3]{0:T(128)}, u32[]{:S(2)}) copy-start(s32[3]{0:T(128)} %constant.125) | copy-start | bytes 40
  305.6 98.4 %copy-start.53 = (s32[3]{0:T(128)S(1)}, s32[3]{0:T(128)}, u32[]{:S(2)}) copy-start(s32[3]{0:T(128)} %constant.128) | copy-start | bytes 40
  305.6 190.7 %copy-start.52 = (bf16[384]{0:T(512)(128)(2,1)S(1)}, bf16[384]{0:T(512)(128)(2,1)}, u32[]{:S(2)}) copy-start(bf16[384]{0:T(512)(128)(2,1)} %param.34) | copy-start | bytes 2308
  305.7 190.8 %copy-start.51 = (u32[32]{0:T(128)S(1)}, u32[32]{0:T(128)}, u32[]{:S(2)}) copy-start(u32[32]{0:T(128)} %constant.300) | copy-start | bytes 388
  305.7 192.0 %copy-start.56 = (bf16[96]{0:T(256)(128)(2,1)S(1)}, bf16[96]{0:T(256)(128)(2,1)}, u32[]{:S(2)}) copy-start(bf16[96]{0:T(256)(128)(2,1)} %param.38) | copy-start | bytes 580
  305.7 192.2 %copy-start.57 = (bf16[96]{0:T(256)(128)(2,1)S(1)}, bf16[96]{0:T(256)(128)(2,1)}, u32[]{:S(2)}) copy-start(bf16[96]{0:T(256)(128)(2,1)} %param.36) | copy-start | bytes 580
  305.7 192.5 %copy-start.58 = (bf16[96]{0:T(256)(128)(2,1)S(1)}, bf16[96]{0:T(256)(128)(2,1)}, u32[]{:S(2)}) copy-start(bf16[96]{0:T(256)(128)(2,1)} %param.31) | copy-start | bytes 580
  305.7 192.7 %copy-start.59 = (bf16[96]{0:T(256)(128)(2,1)S(1)}, bf16[96]{0:T(256)(128)(2,1)}, u32[]{:S(2)}) copy-start(bf16[96]{0:T(256)(128)(2,1)} %param.32) | copy-start | bytes 580
  305.7 192.9 %copy-start.60 = (bf16[96]{0:T(256)(128)(2,1)S(1)}, bf16[96]{0:T(256)(128)(2,1)}, u32[]{:S(2)}) copy-start(bf16[96]{0:T(256)(128)(2,1)} %param.30) | copy-start | bytes 580
  305.7 193.1 %copy-start.61 = (bf16[96]{0:T(256)(128)(2,1)S(1)}, bf16[96]{0:T(256)(128)(2,1)}, u32[]{:S(2)}) copy-start(bf16[96]{0:T(256)(128)(2,1)} %param.28) | copy-start | bytes 580
  305.7 193.4 %copy-start.62 = (bf16[96]{0:T(256)(128)(2,1)S(1)}, bf16[96]{0:T(256)(128)(2,1)}, u32[]{:S(2)}) copy-start(bf16[96]{0:T(256)(128)(2,1)} %param.27) | copy-start | bytes 580
  305.8 193.6 %copy-start.63 = (bf16[96]{0:T(256)(128)(2,1)S(1)}, bf16[96]{0:T(256)(128)(2,1)}, u32[]{:S(2)}) copy-start(bf16[96]{0:T(256)(128)(2,1)} %param.37) | copy-start | bytes 580
  403.0 164.4 %copy-start.25 = (bf16[1,1024,768]{2,1,0:T(8,128)(2,1)S(1)}, bf16[1,1024,768]{2,1,0:T(8,128)(2,1)}, u32[]{:S(2)}) copy-start(bf16[1,1024,768]{2,1,0:T(8,128)(2,1)} %param.43) | copy-start | bytes 4718596
  403.2 581.9 %copy-start.32 = (s32[1,12,1024]{2,0,1:T(1,128)}, s32[1,12,1024]{2,0,1:T(1,128)S(1)}, u32[]{:S(2)}) copy-start(s32[1,12,1024]{2,0,1:T(1,128)S(1)} %get-tuple-element.108) | copy-start | bytes 147460
  403.4 581.7 %copy-start.34 = (s32[1,12,1024]{2,0,1:T(1,128)}, s32[1,12,1024]{2,0,1:T(1,128)S(1)}, u32[]{:S(2)}) copy-start(s32[1,12,1024]{2,0,1:T(1,128)S(1)} %get-tuple-element.106) | copy-start | bytes 147460
  496.3 619.7 %copy-start.37 = (pred[12,1024]{1,0:T(8,128)(4,1)}, pred[12,1024]{1,0:T(8,128)(4,1)S(1)}, u32[]{:S(2)}) copy-start(pred[12,1024]{1,0:T(8,128)(4,1)S(1)} %and_bitcast_fusion.1) | copy-start | bytes 36868
  566.1 400.4 %copy-start.39 = (pred[1,12,1024,1]{2,1,3,0:T(8,128)(4,1)}, pred[1,12,1024,1]{2,1,3,0:T(8,128)(4,1)S(1)}, u32[]{:S(2)}) copy-start(pred[1,12,1024,1]{2,1,3,0:T(8,128)(4,1)S(1)} %copy.184) | copy-start | bytes 36868
  566.4 418.6 %copy-start.41 = (pred[12,8,128]{2,1,0:T(8,128)(4,1)}, pred[12,8,128]{2,1,0:T(8,128)(4,1)S(1)}, u32[]{:S(2)}) copy-start(pred[12,8,128]{2,1,0:T(8,128)(4,1)S(1)} %slice.147) | copy-start | bytes 36868
  566.7 418.4 %copy-start.43 = (pred[12,8,128]{2,1,0:T(8,128)(4,1)}, pred[12,8,128]{2,1,0:T(8,128)(4,1)S(1)}, u32[]{:S(2)}) copy-start(pred[12,8,128]{2,1,0:T(8,128)(4,1)S(1)} %slice.148) | copy-start | bytes 36868
  567.4 426.0 %copy-start.5 = (s32[12288]{0:T(1024)}, s32[12288]{0:T(1024)S(1)}, u32[]{:S(2)}) copy-start(s32[12288]{0:T(1024)S(1)} %reshape.741) | copy-start | bytes 147460
  1121.5 39.1 %copy-start.10 = (f32[1024,768]{0,1:T(8,128)}, f32[1024,768]{0,1:T(8,128)S(1)}, u32[]{:S(2)}) copy-start(f32[1024,768]{0,1:T(8,128)S(1)} %get-tuple-element.122) | copy-start | bytes 9437188
  1122.0 38.7 %copy-start.50 = (f32[768]{0:T(1024)S(1)}, f32[768]{0:T(1024)}, u32[]{:S(2)}) copy-start(f32[768]{0:T(1024)} %convert_element_type.127) | copy-start | bytes 9220
  1865.7 28.9 copy-start.48
  (42 other events, 254.3 us)
Sparse Core Ops, SparseCore 0:
  10.2 67.8 all-gather.5
  80.3 39.5 all-gather.7
  122.1 78.6 all-gather.9
  202.8 78.0 all-gather.11
  2974.3 74.5 all-reduce.12
where the time goes:
time: 3100 us; the launch traced here: 3090 us
  local copies, waits for them, and re-layouts  1660 us (54%)
  blocking collectives  1130 us (36%)
  matrix products  172 us (6%)
  waiting for transfers between devices  66.3 us (2%)
  other arithmetic  40.3 us (1%)
    unnamed x2, blocking collectives  1110 us
    gather x18, local copies, waits for them, and re-layouts, arrange(): return jnp.take_along_axis(tensor, order[..., None], axis=2)  987 us
    unnamed x186, local copies, waits for them, and re-layouts  185 us
    gather x1, local copies, waits for them, and re-layouts, shards(): ok_query = jnp.take_along_axis(ok_heads, query_perm, axis=2).reshape(cshape)  97.2 us
    gather x1, local copies, waits for them, and re-layouts, shards(): jnp.take_along_axis(seg_heads, query_perm, axis=2).reshape(cshape)  97.2 us
    gather x1, local copies, waits for them, and re-layouts, shards(): ok_key = jnp.take_along_axis(ok_heads, key_perm, axis=2).reshape(cshape)  97.2 us
    gather x1, local copies, waits for them, and re-layouts, shards(): seg_key = jnp.take_along_axis(seg_heads, key_perm, axis=2).reshape(cshape)  97.2 us
    psum x1, waiting for transfers between devices, shards(): my_rows = lax.psum(my_rows.astype(jnp.bfloat16), 'rep').astype(jnp.float32)  63.7 us
  transfers between devices with their start and end apart: 5, of which 1 were waited for; matrix products, arithmetic and copies ran while one was open for 35% of the time, Pallas kernels for 0%

commit v1 on v0

v1 whole, which is shorter than its diff:
```python
from functools import partial

import jax
import jax.numpy as jnp
from jax import lax
from jax.experimental import pallas as pl
from jax.experimental.pallas import tpu as pltpu
from jax.sharding import PartitionSpec as P

CL = 128
EPS = 1e-06
BIG = 2.0**100
F32 = jnp.float32
BF16 = jnp.bfloat16
NN = (((1,), (0,)), ((), ()))
NT = (((1,), (1,)), ((), ()))
TN = (((0,), (0,)), ((), ()))
TT = (((0,), (1,)), ((), ()))


def mm(a, b, dims):
    return lax.dot_general(a, b, dims, preferred_element_type=F32)


def rows2(value):
    return value.reshape(value.shape[0] * value.shape[1] * value.shape[2], value.shape[3])


def norm_parts(resid):
    average = jnp.mean(resid, axis=-1, keepdims=True)
    centred = resid - average
    variance = jnp.mean(centred * centred, axis=-1, keepdims=True)
    inv_std = lax.rsqrt(variance + EPS)
    return centred * inv_std, inv_std


def norm_back(grad_out, normed, inv_std, gain):
    scaled = grad_out * gain
    first_term = jnp.mean(scaled, axis=-1, keepdims=True)
    second_term = jnp.mean(scaled * normed, axis=-1, keepdims=True)
    return inv_std * (scaled - first_term - normed * second_term)


def gelu_both(z):
    gauss = jnp.exp(-0.5 * (z * z))
    t = 1.0 / (1.0 + (0.3275911 * 0.7071067811865476) * jnp.abs(z))
    poly = t * (0.127414796 + t * (-0.142248368 + t * (0.7107068705 + t * (-0.7265760135 + t * 0.5307027145))))
    tail = poly * gauss
    phi = jnp.where(z >= 0.0, 1.0 - tail, tail)
    return z * phi, phi + z * gauss * 0.3989422804014327


def one_hot(perm_ref, h, pt_ref):
    length = pt_ref.shape[0]
    row = perm_ref[pl.ds(h, 1), :].astype(jnp.int16)
    places = lax.broadcasted_iota(jnp.int16, (length, length), 0)
    pt_ref[...] = jnp.where(places == row, jnp.ones((), BF16), jnp.zeros((), BF16))


def fwd_kernel(
    heads,
    x_hbm, w_in_hbm, w_out_hbm, w_inner_hbm, w_outer_hbm, vec_ref, seg_ref, ok_ref, qperm_ref, kperm_ref, cot_hbm,
    hid_hbm, act_hbm, din_hbm, flow_hbm, dou_hbm, dfi_hbm, dbr_hbm, att_hbm, head_hbm, xt_hbm, vgrad_ref,
    xv, cot, w_in, w_out, w_inner, w_outer, qkv, qcode, kcode, ptq, ptk, att, head, xt,
    act, din, flow, dou, dfi, dbr, hid, gp, fo, nf, ds,
    in_sem, out_sem, head_sem,
):
    length, width = xv.shape
    hd = width // heads
    ff = act.shape[-1]
    tm = act.shape[1]
    fc = width
    n_in = 3 * width

    loads = [
        pltpu.make_async_copy(s, d, in_sem.at[i])
        for i, (s, d) in enumerate(
            ((x_hbm, xv), (w_in_hbm, w_in), (w_out_hbm, w_out), (w_inner_hbm, w_inner), (w_outer_hbm, w_outer), (cot_hbm, cot))
        )
    ]
    for load in loads:
        load.start()
    vec = vec_ref[...].astype(F32)
    vec_t = vec.T

    code_rows = lax.broadcasted_iota(jnp.int32, (16, length), 0)
    seg = seg_ref[...]
    ok = ok_ref[...] > 0
    qcode[...] = jnp.where(code_rows == jnp.where(ok, seg, 4), 1.0, 0.0).astype(BF16)
    kcode[...] = jnp.where((code_rows < 5) & (code_rows != jnp.where(ok, seg, 5)), -BIG, 0.0).astype(BF16)

    loads[0].wait()
    xt[...] = xv[...].T
    loads[1].wait()
    nt = 256
    for i in range(n_in // nt):
        n0 = i * nt
        acc = mm(rows2(w_in[:, :, :, n0 : n0 + nt]), xv[...], TT)
        if n0 < width:
            acc = (acc + vec_t[n0 : n0 + nt, 0:1]).astype(BF16) * 0.125
        elif n0 >= 2 * width:
            acc = acc + vec_t[n0 - 2 * width : n0 - 2 * width + nt, 1:2]
        qkv[n0 : n0 + nt, :] = acc.astype(BF16)

    def attend(h):
        r0 = pl.multiple_of(h * hd, hd)
        rows = pl.ds(r0, hd)
        one_hot(qperm_ref, h, ptq)
        one_hot(kperm_ref, h, ptk)
        q_side = jnp.concatenate([qkv[rows, :], qcode[...]], axis=0)
        k_side = jnp.concatenate(
            [qkv[pl.ds(pl.multiple_of(width + r0, hd), hd), :], kcode[...], qkv[pl.ds(pl.multiple_of(2 * width + r0, hd), hd), :]],
            axis=0,
        )
        q_arr = mm(q_side, ptq[...], NN).astype(BF16)
        k_arr = mm(k_side, ptk[...], NN).astype(BF16)
        v_arr = k_arr[hd + 16 :, :]
        head[h, :hd, :] = q_arr[:hd, :]
        head[h, hd : 2 * hd, :] = k_arr[:hd, :]
        head[h, 2 * hd : 3 * hd, :] = v_arr
        cols = [slice(c * CL, (c + 1) * CL) for c in range(length // CL)]
        scores = jnp.concatenate([mm(k_arr[: hd + 16, c], q_arr[:, c], TN) for c in cols], axis=1)
        top = jnp.maximum(jnp.max(scores, axis=0, keepdims=True), -1e29)
        raised = jnp.exp(scores - top)
        total = jnp.maximum(jnp.sum(raised, axis=0, keepdims=True), 1.0)
        probs = (raised * (1.0 / total)).astype(BF16)
        head[h, 3 * hd :, :] = probs
        combined = jnp.concatenate([mm(v_arr[:, c], probs[:, c], NN) for c in cols], axis=1)
        att[rows, :] = mm(combined.astype(BF16), ptq[...], NT).astype(BF16)

    @pl.loop(0, heads)
    def _(h):
        attend(h)

    heads_out = [
        pltpu.make_async_copy(s, d, head_sem.at[i])
        for i, (s, d) in enumerate(((att, att_hbm), (head, head_hbm), (xt, xt_hbm)))
    ]
    for copy in heads_out:
        copy.start()
    for load in loads[2:]:
        load.wait()

    b_out, g_first, s_first = vec[2:3, :], vec[3:4, :], vec[4:5, :]
    b_outer, g_second, s_second = vec[5:6, :], vec[6:7, :], vec[7:8, :]
    vgrad_ref[...] = jnp.zeros_like(vgrad_ref)

    def add_row(row, value):
        vgrad_ref[row : row + 1, :] += jnp.sum(value, axis=0, keepdims=True)

    def outs(i, slot):
        rows = pl.ds(pl.multiple_of(i * tm, tm), tm)
        return [
            pltpu.make_async_copy(s.at[slot], d.at[rows, :], out_sem.at[slot, n])
            for n, (s, d) in enumerate(
                ((act, act_hbm), (din, din_hbm), (flow, flow_hbm), (dou, dou_hbm), (dfi, dfi_hbm), (dbr, dbr_hbm), (hid, hid_hbm))
            )
        ]

    n_tiles = length // tm

    @pl.loop(0, n_tiles)
    def _(i):
        slot = lax.rem(i, 2)
        t0 = pl.multiple_of(i * tm, tm)
        rows = pl.ds(t0, tm)

        @pl.when(i >= 2)
        def _():
            for copy in outs(i - 2, slot):
                copy.wait()

        branch = mm(att[:, rows], rows2(w_out[...]), TN)
        first_sum = xv[rows, :].astype(F32) + branch + b_out
        normed, inv_first = norm_parts(first_sum)
        nf[...] = normed
        first_out = normed * g_first + s_first
        fo[...] = first_out
        flow[slot] = first_out.astype(BF16)
        outer = None
        for j in range(ff // fc):
            cols = slice(j * fc, (j + 1) * fc)
            inner = mm(flow[slot], rows2(w_inner[:, :, :, cols]), NN) + vec[8 + j : 9 + j, :]
            high, slope = gelu_both(inner)
            act[slot, :, cols] = high.astype(BF16)
            gp[:, cols] = slope
            per = w_outer.shape[0] * fc // ff
            term = mm(act[slot, :, cols], rows2(w_outer[j * per : (j + 1) * per]), NN)
            outer = term if outer is None else outer + term
        normed_second, inv_second = norm_parts(fo[...] + outer + b_outer)
        hid[slot] = (normed_second * g_second + s_second).astype(BF16)
        grad = cot[rows, :].astype(F32)
        d_second = norm_back(grad, normed_second, inv_second, g_second)
        add_row(6, grad * normed_second)
        add_row(7, grad)
        ds[...] = d_second
        low = d_second.astype(BF16)
        dou[slot] = low
        add_row(5, low.astype(F32))
        back = None
        for j in range(ff // fc):
            cols = slice(j * fc, (j + 1) * fc)
            per = w_outer.shape[0] * fc // ff
            d_act = mm(dou[slot], rows2(w_outer[j * per : (j + 1) * per]), NT)
            d_inner = (d_act * gp[:, cols]).astype(BF16)
            din[slot, :, cols] = d_inner
            add_row(8 + j, d_inner.astype(F32))
            term = mm(d_inner, rows2(w_inner[:, :, :, cols]), NT)
            back = term if back is None else back + term
        d_first_out = ds[...] + back
        normed = nf[...]
        add_row(3, d_first_out * normed)
        add_row(4, d_first_out)
        d_first = norm_back(d_first_out, normed, inv_first, g_first)
        dfi[slot] = d_first
        low = d_first.astype(BF16)
        dbr[slot] = low
        add_row(2, low.astype(F32))
        for copy in outs(i, slot):
            copy.start()

    for i in range(max(0, n_tiles - 2), n_tiles):
        for copy in outs(i, i % 2):
            copy.wait()
    for copy in heads_out:
        copy.wait()


def fwd_call(x, w_in, w_out, w_inner, w_outer, vec, seg, ok, qperm, kperm, cot):
    length, width = x.shape
    heads = qperm.shape[0]
    hd = width // heads
    ff = w_inner.shape[-1]
    tm = 256
    hbm = pl.BlockSpec(memory_space=pl.ANY)
    vmem = pl.BlockSpec(memory_space=pltpu.VMEM)
    outs = [
        ((length, width), BF16), ((length, ff), BF16), ((length, ff), BF16), ((length, width), BF16), ((length, width), BF16),
        ((length, width), F32), ((length, width), BF16), ((width, length), BF16), ((heads, 3 * hd + CL, length), BF16),
        ((width, length), BF16), ((16, width), F32),
    ]
    scratch = [
        ((length, width), BF16), ((length, width), BF16), (w_in.shape, BF16), (w_out.shape, BF16), (w_inner.shape, BF16), (w_outer.shape, BF16),
        ((3 * width, length), BF16), ((16, length), BF16), ((16, length), BF16), ((length, length), BF16), ((length, length), BF16),
        ((width, length), BF16), ((heads, 3 * hd + CL, length), BF16), ((width, length), BF16),
        ((2, tm, ff), BF16), ((2, tm, ff), BF16), ((2, tm, width), BF16), ((2, tm, width), BF16), ((2, tm, width), F32), ((2, tm, width), BF16),
        ((2, tm, width), BF16), ((tm, ff), F32), ((tm, width), F32), ((tm, width), F32), ((tm, width), F32),
    ]
    return pl.pallas_call(
        partial(fwd_kernel, heads),
        out_shape=[jax.ShapeDtypeStruct(s, d) for s, d in outs],
        in_specs=[hbm] * 5 + [vmem] * 5 + [hbm],
        out_specs=[hbm] * 10 + [vmem],
        scratch_shapes=[pltpu.VMEM(s, d) for s, d in scratch]
        + [pltpu.SemaphoreType.DMA((6,)), pltpu.SemaphoreType.DMA((2, 7)), pltpu.SemaphoreType.DMA((3,))],
        compiler_params=pltpu.CompilerParams(vmem_limit_bytes=60 << 20),
        name="layer_forward",
    )(x, w_in, w_out, w_inner, w_outer, vec, seg, ok, qperm, kperm, cot)


HG = 4


def bwd_kernel(
    heads,
    act_hbm, din_hbm, flow_hbm, dou_hbm, dfi_hbm, dbr_hbm, att_hbm, head_hbm, xt_hbm, w_in_hbm, w_out_hbm, qperm_ref, kperm_ref, vg_ref,
    ig_hbm, g_in_hbm, g_out_hbm, g_inner_hbm, g_outer_hbm, vgrad_ref,
    act, din, flow, dou, dfi, dbr, att, head, xt, w_in, w_out, ptq, ptk, mixed, dproj, g_in, g_out, g_inner, g_outer, ig,
    in_sem, act_sem, din_sem, head_sem, dfi_sem, out_sem,
):
    length, width = flow.shape
    hd = width // heads
    tm = ig.shape[1]
    fc = act.shape[2]
    ic = din.shape[2]
    copy = pltpu.make_async_copy
    n_act = act_hbm.shape[1] // fc
    n_din = din_hbm.shape[1] // ic
    n_tiles = length // tm
    acts = [copy(act_hbm.at[:, j * fc : (j + 1) * fc], act.at[j % 2], act_sem.at[j % 2]) for j in range(n_act)]
    dins = [copy(din_hbm.at[:, j * ic : (j + 1) * ic], din.at[j % 2], din_sem.at[j % 2]) for j in range(n_din)]
    dfis = [copy(dfi_hbm.at[i * tm : (i + 1) * tm, :], dfi.at[i % 2], dfi_sem.at[i % 2]) for i in range(n_tiles)]
    loads = {
        name: copy(s, d, in_sem.at[i])
        for i, (name, s, d) in enumerate(
            (
                ("dou", dou_hbm, dou), ("flow", flow_hbm, flow), ("dbr", dbr_hbm, dbr), ("w_out", w_out_hbm, w_out),
                ("att", att_hbm, att), ("xt", xt_hbm, xt.at[:width, :]), ("w_in", w_in_hbm, w_in),
            )
        )
    }

    def head_copy(h, slot):
        return copy(head_hbm.at[h], head.at[slot], head_sem.at[slot])

    loads["dou"].start()
    acts[0].start()
    acts[1].start()
    loads["flow"].start()
    dins[0].start()
    dins[1].start()
    for name in ("dbr", "w_out", "att", "xt", "w_in"):
        loads[name].start()
    head_copy(0, 0).start()
    dfis[0].start()
    dfis[1].start()

    loads["dou"].wait()
    for j in range(n_act):
        acts[j].wait()
        part = mm(act[j % 2], dou[...], TN)
        g_outer[j] = part.astype(BF16).reshape(g_outer.shape[1:])
        if j + 2 < n_act:
            acts[j + 2].start()

    loads["flow"].wait()
    mixed[...] = flow[...].T
    for j in range(n_din):
        dins[j].wait()
        part = mm(mixed[...], din[j % 2], NN)
        g_inner[:, :, :, j * ic : (j + 1) * ic] = part.astype(BF16).reshape(g_inner.shape[:3] + (ic,))
        if j + 2 < n_din:
            dins[j + 2].start()

    for name in ("dbr", "w_out", "att"):
        loads[name].wait()
    mixed[...] = mm(rows2(w_out[...]), dbr[...], NT).astype(BF16)
    g_out[...] = mm(att[...], dbr[...], NN).astype(BF16).reshape(g_out.shape)

    cols = [slice(c * CL, (c + 1) * CL) for c in range(length // CL)]

    def attend(h):
        slot = lax.rem(h, 2)
        one_hot(qperm_ref, h, ptq)
        one_hot(kperm_ref, h, ptk)
        r0 = pl.multiple_of(h * hd, hd)
        d_arr = mm(mixed[pl.ds(r0, hd), :], ptq[...], NN).astype(BF16)
        head_copy(h, slot).wait()

        @pl.when(h + 1 < heads)
        def _():
            head_copy(h + 1, 1 - slot).start()

        q_arr = head[slot, :hd, :]
        k_arr = head[slot, hd : 2 * hd, :]
        v_arr = head[slot, 2 * hd : 3 * hd, :]
        probs = head[slot, 3 * hd :, :]
        d_probs = jnp.concatenate([mm(v_arr[:, c], d_arr[:, c], TN) for c in cols], axis=1)
        wide = probs.astype(F32)
        terms = jnp.sum(wide * d_probs, axis=0, keepdims=True)
        d_scores = (wide * (d_probs - terms)).astype(BF16)
        dq = jnp.concatenate([mm(k_arr[:, c], d_scores[:, c], NN) for c in cols], axis=1) * 0.125
        dk = jnp.concatenate([mm(q_arr[:, c], d_scores[:, c], NT) for c in cols], axis=1)
        dv = jnp.concatenate([mm(d_arr[:, c], probs[:, c], NT) for c in cols], axis=1)
        dproj[pl.ds(r0, hd), :] = mm(dq.astype(BF16), ptq[...], NT).astype(BF16)
        dkv = mm(jnp.concatenate([dk, dv], axis=0).astype(BF16), ptk[...], NT).astype(BF16)
        dproj[pl.ds(pl.multiple_of(width + r0, hd), hd), :] = dkv[:hd, :]
        dproj[pl.ds(pl.multiple_of(2 * width + r0, hd), hd), :] = dkv[hd:, :]

    loads["xt"].wait()
    xt[width:, :] = jnp.where(lax.broadcasted_iota(jnp.int32, (16, length), 0) == 0, 1.0, 0.0).astype(BF16)
    vgrad_ref[...] = vg_ref[...]
    gw = HG * hd
    for g in range(heads // HG):
        @pl.loop(g * HG, (g + 1) * HG)
        def _(h):
            attend(h)

        for part in range(3):
            c0 = part * width + g * gw
            prod = mm(xt[...], dproj[c0 : c0 + gw, :], NT)
            g_in[g, :, :, :, part * gw : (part + 1) * gw] = prod[:width].astype(BF16).reshape(g_in.shape[1:4] + (gw,))
            if part != 1:
                vgrad_ref[part // 2 : part // 2 + 1, g * gw : (g + 1) * gw] = prod[width : width + 1]

    outs = [
        copy(s, d, out_sem.at[i])
        for i, (s, d) in enumerate(((g_in, g_in_hbm), (g_out, g_out_hbm), (g_inner, g_inner_hbm), (g_outer, g_outer_hbm)))
    ]
    for out in outs:
        out.start()
    loads["w_in"].wait()
    stores = [copy(ig.at[i % 2], ig_hbm.at[i * tm : (i + 1) * tm, :], out_sem.at[4 + i % 2]) for i in range(n_tiles)]
    for i in range(n_tiles):
        prod = mm(rows2(w_in[...]), dproj[:, i * tm : (i + 1) * tm], NN)
        dfis[i].wait()
        if i >= 2:
            stores[i - 2].wait()
        ig[i % 2] = (dfi[i % 2] + prod.T).astype(BF16)
        stores[i].start()
        if i + 2 < n_tiles:
            dfis[i + 2].start()
    for i in range(max(0, n_tiles - 2), n_tiles):
        stores[i].wait()
    for out in outs:
        out.wait()


def bwd_call(act, din, flow, dou, dfi, dbr, att, head, xt, w_in, w_out, qperm, kperm, vgrad):
    length, width = flow.shape
    heads = qperm.shape[0]
    hd = width // heads
    ff = act.shape[1]
    tm = 256
    hbm = pl.BlockSpec(memory_space=pl.ANY)
    vmem = pl.BlockSpec(memory_space=pltpu.VMEM)
    blocks = w_in.shape[:3]
    gshapes = [(heads // HG,) + blocks + (3 * HG * hd,), blocks + (width,), blocks + (ff,), (8, 2, ff // 16, width)]
    fc = ff // 8
    outs = [((length, width), BF16)] + [(s, BF16) for s in gshapes] + [((16, width), F32)]
    scratch = [
        ((2, length, fc), BF16), ((2, length, width), BF16), ((length, width), BF16), ((length, width), BF16), ((2, tm, width), F32),
        ((length, width), BF16), ((width, length), BF16), ((2,) + head.shape[1:], BF16), ((width + 16, length), BF16), (w_in.shape, BF16), (w_out.shape, BF16),
        ((length, length), BF16), ((length, length), BF16), ((width, length), BF16), ((3 * width, length), BF16),
    ] + [(s, BF16) for s in gshapes] + [((2, tm, width), BF16)]
    return pl.pallas_call(
        partial(bwd_kernel, heads),
        out_shape=[jax.ShapeDtypeStruct(s, d) for s, d in outs],
        in_specs=[hbm] * 11 + [vmem] * 3,
        out_specs=[hbm] * 5 + [vmem],
        scratch_shapes=[pltpu.VMEM(s, d) for s, d in scratch]
        + [pltpu.SemaphoreType.DMA((n,)) for n in (7, 2, 2, 2, 2, 6)],
        compiler_params=pltpu.CompilerParams(vmem_limit_bytes=60 << 20),
        name="layer_backward",
    )(act, din, flow, dou, dfi, dbr, att, head, xt, w_in, w_out, qperm, kperm, vgrad)


def shards(
    layer_input, in_weight, query_bias, value_bias, out_weight, out_bias, first_gain, first_shift, inner_weight, inner_bias,
    outer_weight, outer_bias, second_gain, second_shift, segment_ids, token_valid, query_perm, key_perm, out_cotangent,
):
    _, length, width = layer_input.shape
    heads = query_perm.shape[1]
    ff = inner_weight.shape[1]
    n_shard = lax.axis_size("shard")
    shard = lax.axis_index("shard")

    def whole(rows):
        return lax.all_gather(rows, "shard", axis=0, tiled=True)

    def blocked(rows):
        return rows.reshape(8, 2, rows.shape[0] // 16, rows.shape[1])

    w_in, w_out, w_inner, w_outer = [blocked(whole(w)) for w in (in_weight, out_weight, inner_weight, outer_weight)]
    short = jnp.stack([query_bias, value_bias, out_bias, first_gain, first_shift, outer_bias, second_gain, second_shift])
    vectors = lax.all_gather(jnp.concatenate([short.reshape(-1), inner_bias]), "shard", axis=0)
    piece = width // n_shard
    vec = jnp.concatenate(
        [
            jnp.transpose(vectors[:, : 8 * piece].reshape(n_shard, 8, piece), (1, 0, 2)).reshape(8, width),
            vectors[:, 8 * piece :].reshape(ff // width, width),
            jnp.zeros((8 - ff // width, width), BF16),
        ]
    )
    hidden, act, din, flow, dou, dfi, dbr, att, head, xt, vg = fwd_call(
        layer_input[0], w_in, w_out, w_inner, w_outer, vec, segment_ids, token_valid, query_perm[0], key_perm[0], out_cotangent[0]
    )
    grad_x, g_in, g_out, g_inner, g_outer, vg = bwd_call(
        act, din, flow, dou, dfi, dbr, att, head, xt, w_in, w_out, query_perm[0], key_perm[0], vg
    )
    groups = heads // HG
    g_in = jnp.transpose(g_in.reshape(groups, width, 3, width // groups), (1, 2, 0, 3)).reshape(width, 3 * width)
    grads = [g_in, g_out.reshape(width, width), g_inner.reshape(width, ff), g_outer.reshape(ff, width)]

    def summed(grad):
        rows = lax.psum_scatter(grad.astype(F32), "shard", scatter_dimension=0, tiled=True)
        return lax.psum(rows.astype(BF16), "rep").astype(F32)

    d_in, d_out, d_inner, d_outer = [summed(g) for g in grads]
    vg = lax.psum(vg, ("rep", "shard"))
    mine = lax.dynamic_slice(vg, (0, shard * piece), (8, piece))
    inner_piece = ff // n_shard
    inner_mine = lax.dynamic_slice(vg[8 : 8 + ff // width].reshape(ff), (shard * inner_piece,), (inner_piece,))
    return (
        hidden[None], grad_x[None], d_in, mine[0], mine[1], d_out, mine[2], mine[3], mine[4], d_inner, inner_mine, d_outer,
        mine[5], mine[6], mine[7],
    )


def solution(mesh):
    rows, vector = P("shard", None), P("shard")
    seq2, seq3 = P(("rep", "shard"), None), P(("rep", "shard"), None, None)
    return jax.shard_map(
        shards,
        mesh=mesh,
        in_specs=(
            seq3, rows, vector, vector, rows, vector, vector, vector, rows, vector, rows, vector, vector, vector, seq2, seq2, seq3, seq3, seq3,
        ),
        out_specs=(seq3, seq3, rows, vector, vector, rows, vector, vector, vector, rows, vector, rows, vector, vector, vector),
        check_vma=False,
    )
```

time: 3100 us -> 1030 us (0.33)
  local copies, waits for them, and re-layouts: 1660 us -> 35.1 us
  blocking collectives: 1130 us -> 72.7 us
  waiting for transfers between devices: 66.3 us -> 732 us
  matrix products: 172 us -> 0 us
  Pallas kernels: 0 us -> 142 us
    gather x22 -> x0, local copies, waits for them, and re-layouts: 1380 us -> none  [the longest x18 987 us: arrange(): return jnp.take_along_axis(tensor, order[..., None], axis=2)]
    unnamed x2 -> x0, blocking collectives: 1110 us -> none
    reduce_scatter x0 -> x3, waiting for transfers between devices: none -> 355 us  [summed(): lax.psum_scatter(grad.astype(F32), 'shard', scatter_dimension=0, tiled=True)]
    all_gather x4, waiting for transfers between devices: 0.02 us -> 234 us  [whole(): return lax.all_gather(rows, 'shard', axis=0, tiled=True)]
    unnamed x186 -> x12, local copies, waits for them, and re-layouts: 185 us -> 14.1 us
    dot_general x16 -> x0, matrix products: 156 us -> none  [the longest x1 38.7 us: shards(): jnp.dot(first_low, w_inner, preferred_element_type=jnp.float32)]
    pallas_call x0 -> x2, Pallas kernels: none -> 142 us  [the longest x1 73.1 us: bwd_call(): pl.pallas_call(partial(bwd_kernel, heads), out_shape=[jax.ShapeDtypeStruc...]
    unnamed x5 -> x10, waiting for transfers between devices: 2.6 us -> 133 us
  transfers between devices with their start and end apart: 5 -> 9, of which waited for: 1 -> 9; matrix products, arithmetic and copies ran while one was open for 35% -> 5% of each run, Pallas kernels for 0% -> 0%
where the time goes in v1:
time: 1030 us
  waiting for transfers between devices  732 us (71%)
  Pallas kernels  142 us (14%)
  blocking collectives  72.7 us (7%)
  local copies, waits for them, and re-layouts  35.1 us (3%)
  other arithmetic  29.3 us (3%)
  between operations  14.1 us (1%)
    reduce_scatter x3, waiting for transfers between devices, summed(): lax.psum_scatter(grad.astype(F32), 'shard', scatter_dimension=0, tiled=True)  355 us
    all_gather x4, waiting for transfers between devices, whole(): return lax.all_gather(rows, 'shard', axis=0, tiled=True)  234 us
    unnamed x10, waiting for transfers between devices  133 us
    pallas_call x1, Pallas kernels, bwd_call(): pl.pallas_call(partial(bwd_kernel, heads), out_shape=[jax.ShapeDtypeStruc...  73.1 us
    pallas_call x1, Pallas kernels, fwd_call(): pl.pallas_call(partial(fwd_kernel, heads), out_shape=[jax.ShapeDtypeStruc...  69 us
    psum x1, blocking collectives, shards(): vg = lax.psum(vg, ('rep', 'shard'))  40.3 us
    all_gather x1, blocking collectives, shards(): lax.all_gather(jnp.concatenate([short.reshape(-1), inner_bias]), 'shard',...  32.4 us
  transfers between devices with their start and end apart: 9, of which 9 were waited for; matrix products, arithmetic and copies ran while one was open for 5% of the time, Pallas kernels for 0%

profile of v1, /device:TPU:0, one launch (start us, length us, event | category | flops | bytes accessed | tf_op | source)
XLA Modules:
  0.0 1025.2 jit_solution(13049223179126365812)
XLA Ops:
  8.0 0.7 all-gather.7.cloned.1.call-update
  10.0 0.8 stack.35
  10.9 0.7 pad_maximum_fusion
  11.6 32.4 %all-gather.1 = bf16[8,1,1152]{2,1,0:T(2,128)(2,1)S(1)} all-gather(bf16[1,1,1152]{2,1,0:T(2,128)(2,1)S(1)} %reshape.87), channel_id=2, replica_groups=mesh['rep'=4,'shard'=8] {'shard'}, dimensions={0}, use_global_device_ids=true | all-gather | bytes 20736 | tf_op jit(solution)/shard_map/all_gather | solution.py:446
  44.3 0.7 maximum_maximum_fusion.vec_ref
  45.0 1.5 copy_bitcast_fusion
  46.5 7.6 all-gather.9.cloned.1.call-done
  54.1 66.1 %all-gather.7.cloned.1.call-done = bf16[768,2304]{1,0:T(8,128)(2,1)} async-done(((bf16[96,2304]{1,0:T(8,128)(2,1)}), bf16[768,2304]{1,0:T(8,128)(2,1)}) %all-gather.7.cloned.1.call-update) | async-done | bytes 3538960 | tf_op jit(solution)/shard_map/all_gather | solution.py:439
  120.2 80.6 %all-gather.11.cloned.1.call-done = bf16[768,3072]{1,0:T(8,128)(2,1)} async-done(((bf16[96,3072]{1,0:T(8,128)(2,1)}), bf16[768,3072]{1,0:T(8,128)(2,1)}) %all-gather.11.cloned.1.call-update) | async-done | bytes 4718608 | tf_op jit(solution)/shard_map/all_gather | solution.py:439
  200.8 80.1 %all-gather.13.cloned.1.call-done = bf16[3072,768]{1,0:T(8,128)(2,1)} async-done(((bf16[384,768]{1,0:T(8,128)(2,1)}), bf16[3072,768]{1,0:T(8,128)(2,1)}) %all-gather.13.cloned.1.call-update) | async-done | bytes 4718608 | tf_op jit(solution)/shard_map/all_gather | solution.py:439
  280.9 69.0 %layer_forward.1 = (bf16[1024,768]{1,0:T(8,128)(2,1)}, bf16[1024,3072]{1,0:T(8,128)(2,1)}, bf16[1024,3072]{1,0:T(8,128)(2,1)}, bf16[1024,768]{1,0:T(8,128)(2,1)}...) custom-call(bf16[1024,768]{1,0:T(8,128)(2,1)} %bitcast.64, ...), custom_call_target="tpu_custom_call" | custom-call | tf_op jit(solution)/shard_map/layer_forward/pallas_call | solution.py:249
  349.9 73.1 %layer_backward.1 = (bf16[1024,768]{1,0:T(8,128)(2,1)}, bf16[3,8,2,48,768]{4,3,2,1,0:T(8,128)(2,1)}, bf16[8,2,48,768]{3,2,1,0:T(8,128)(2,1)}, bf16[8,2,48,3072]{...) custom-call(bf16[1024,3072]{1,0:T(8,128)(2,1)} %get-tuple-element.33.act_hbm, ...), custom_call_target="tpu_custom_call" | custom-call | tf_op jit(solution)/shard_map/layer_backward/pallas_call | solution.py:416
  423.0 3.0 bitcast_convert_fusion.2
  426.1 7.7 reshape.85
  433.8 10.9 %copy.43 = f32[768,3,3,256]{0,3,2,1:T(8,128)} copy(f32[768,3,3,256]{3,1,0,2:T(4,128)} %bitcast.56) | data formatting | bytes 14155776 | tf_op jit(solution)/shard_map/convert_element_type | solution.py:466
  444.7 8.1 copy.45
  452.9 7.3 bitcast_convert_fusion.1
  460.3 6.7 bitcast_convert_fusion
  467.1 26.3 %reduce-scatter.7.cloned.1.call-done = f32[96,768]{1,0:T(8,128)} async-done(((f32[768,768]{1,0:T(8,128)}), f32[96,768]{1,0:T(8,128)}) %reduce-scatter.7.cloned.1.call-update) | async-done | bytes 294928 | tf_op jit(solution)/shard_map/reduce_scatter | solution.py:466
  493.4 1.6 convert_element_type.62
  495.0 130.0 %reduce-scatter.13.cloned.1.call-done = f32[96,2304]{1,0:T(8,128)} async-done(((f32[768,2304]{1,0:T(8,128)}), f32[96,2304]{1,0:T(8,128)}) %reduce-scatter.13.cloned.1.call-update) | async-done | bytes 884752
  625.0 2.2 copy.46
  627.2 164.4 %reduce-scatter.9.cloned.1.call-done = f32[96,3072]{1,0:T(8,128)} async-done(((f32[768,3072]{1,0:T(8,128)}), f32[96,3072]{1,0:T(8,128)}) %reduce-scatter.9.cloned.1.call-update) | async-done | bytes 1179664 | tf_op jit(solution)/shard_map/reduce_scatter | solution.py:466
  791.6 2.2 convert_element_type.66
  793.7 164.5 %reduce-scatter.11.cloned.1.call-done = f32[384,768]{1,0:T(8,128)} async-done(((f32[3072,768]{1,0:T(8,128)}), f32[384,768]{1,0:T(8,128)}) %reduce-scatter.11.cloned.1.call-update) | async-done | bytes 1179664 | tf_op jit(solution)/shard_map/reduce_scatter | solution.py:466
  958.2 2.1 convert_element_type.70
  960.4 40.3 %psum.36 = f32[16,768]{1,0:T(8,128)S(1)} all-reduce(f32[16,768]{1,0:T(8,128)S(1)} %copy-done.2), channel_id=1, replica_groups=mesh['rep'=4,'shard'=8] {'rep','shard'}, use_global_device_ids=true, to_apply=%region_2.0 | all-reduce | flops 12288 | bytes 98304 | tf_op jit(solution)/shard_map/psum | solution.py:470
  1002.0 9.4 all-reduce.3.cloned.1.call-done
  1011.3 2.3 copy.44
  1013.6 1.6 convert_element_type.63
  1015.3 2.2 convert_element_type.67
  1017.4 1.1 convert_element_type.71
  (39 shorter events, 4.0 us)
Async XLA Ops:
  7.2 46.9 %all-gather.9.cloned.1.call-start = ((), (), s32[]{:S(2)}) async-start(), calls=%async_computation.5 | async-start | bytes 1327104 | tf_op jit(solution)/shard_map/all_gather | solution.py:439
  7.9 112.3 %all-gather.7.cloned.1.call-start = ((), (), s32[]{:S(2)}) async-start(), calls=%async_computation.4 | async-start | bytes 3981312 | tf_op jit(solution)/shard_map/all_gather | solution.py:439
  8.7 192.1 %all-gather.11.cloned.1.call-start = ((), (), s32[]{:S(2)}) async-start(), calls=%async_computation.6 | async-start | bytes 5308416 | tf_op jit(solution)/shard_map/all_gather | solution.py:439
  9.4 271.5 %all-gather.13.cloned.1.call-start = ((), (), s32[]{:S(2)}) async-start(), calls=%async_computation.7 | async-start | bytes 5308416 | tf_op jit(solution)/shard_map/all_gather | solution.py:439
  10.0 483.4 %reduce-scatter.7.cloned.1.call-start = ((), (), s32[]{:S(2)}) async-start(), calls=%async_computation.8 | async-start | bytes 2654208 | tf_op jit(solution)/shard_map/reduce_scatter | solution.py:466
  423.0 3.1 copy-start
  426.0 198.9 %reduce-scatter.13.cloned.1.call-start = ((), (), s32[]{:S(2)}) async-start(), calls=%async_computation.11 | async-start | bytes 7962624
  452.8 338.8 %reduce-scatter.9.cloned.1.call-start = ((), (), s32[]{:S(2)}) async-start(), calls=%async_computation.9 | async-start | bytes 10616832 | tf_op jit(solution)/shard_map/reduce_scatter | solution.py:466
  460.2 498.0 %reduce-scatter.11.cloned.1.call-start = ((), (), s32[]{:S(2)}) async-start(), calls=%async_computation.10 | async-start | bytes 10616832 | tf_op jit(solution)/shard_map/reduce_scatter | solution.py:466
  467.0 544.3 %all-reduce.3.cloned.1.call-start = ((), (), s32[]{:S(2)}) async-start(), calls=%async_computation.12 | async-start | bytes 3833856 | tf_op jit(solution)/shard_map/psum | solution.py:467
  495.0 465.3 %copy-start.2 = (f32[16,768]{1,0:T(8,128)S(1)}, f32[16,768]{1,0:T(8,128)}, u32[]{:S(2)}) copy-start(f32[16,768]{1,0:T(8,128)} %get-tuple-element.45) | copy-start | bytes 147460
  1011.3 6.1 copy-start.1
Sparse Core Ops, SparseCore 0:
  10.2 43.8 all-gather.8
  56.2 63.9 all-gather.6
  122.4 78.3 all-gather.10
  202.9 78.0 all-gather.12
  426.2 67.1 reduce-scatter.6
  496.9 128.0 reduce-scatter.12
  629.0 162.5 reduce-scatter.8
  795.6 162.5 reduce-scatter.10
  962.1 49.1 all-reduce.2

commit v2 on v1

--- a/solution.py
+++ b/solution.py
@@ -50,6 +50,114 @@
     return z * phi, phi + z * gauss * 0.3989422804014327
 
 
+def rcopy(src, dst, send, recv, axis, index):
+    return pltpu.make_async_remote_copy(
+        src_ref=src, dst_ref=dst, send_sem=send, recv_sem=recv, device_id={axis: index}, device_id_type=pl.DeviceIdType.MESH
+    )
+
+
+class Place:
+    def __init__(self):
+        rep, shard = lax.axis_index("rep"), lax.axis_index("shard")
+        self.x, self.c = rep // 2, rep % 2
+        self.z, self.y = shard // 2, shard % 2
+        self.rep, self.shard = rep, shard
+        self.sibling = self.x * 2 + (1 - self.c)
+        self.across = (1 - self.x) * 2 + self.c
+        self.beside = self.z * 2 + (1 - self.y)
+
+    def plane(self, dz):
+        return (self.z + dz) % 4
+
+    def block(self, dz, dy):
+        return self.plane(dz) * 2 + (self.y + dy) % 2
+
+
+XZ, XY, XX, YZ, YX, YY, CC, OWN, GATHER_SEMS = 0, 4, 8, 16, 20, 24, 28, 36, 37
+
+
+class Gather:
+    def __init__(self, place, source, whole, split, send, recv):
+        self.p, self.source, self.whole, self.send, self.recv = place, source, whole, send, recv
+        self.half = whole.shape[3] // 2
+        start = place.c * self.half
+        self.left = pl.ds(pl.multiple_of(start, 128), split)
+        self.right = pl.ds(pl.multiple_of(start + split, 128), self.half - split)
+        self.mine = pl.ds(pl.multiple_of(start, 128), self.half)
+        self.theirs = pl.ds(pl.multiple_of((1 - place.c) * self.half, 128), self.half)
+        self.started = []
+
+    def go(self, src, dst, sem, axis, index):
+        rcopy(src, dst, self.send.at[sem], self.recv.at[sem], axis, index).start()
+        self.started.append((dst.shape, sem))
+
+    def came(self, dst, sem):
+        rcopy(dst, dst, self.send.at[sem], self.recv.at[sem], "rep", self.p.sibling).wait_recv()
+
+    def own(self):
+        self.own_copy = pltpu.make_async_copy(self.source, self.whole.at[self.p.shard], self.recv.at[OWN])
+        self.own_copy.start()
+
+    def stage_z(self):
+        p = self.p
+        for cols, base in ((self.left, XZ), (self.right, YZ)):
+            for dz in (1, 2, 3):
+                self.go(
+                    self.source.at[p.x, :, cols], self.whole.at[p.shard, p.x, :, cols], base + 4 - dz, "shard", p.plane(dz) * 2 + p.y
+                )
+
+    def stage_second(self):
+        p = self.p
+        own = self.source.at[p.x, :, self.left]
+        self.go(own, self.whole.at[p.shard, p.x, :, self.left], XY, "shard", p.beside)
+        own = self.source.at[:, :, self.right]
+        self.go(own, self.whole.at[p.shard, :, :, self.right], YY, "shard", p.beside)
+        for dz in (1, 2, 3):
+            spot = self.whole.at[p.block(dz, 0), p.x, :, self.left]
+            self.came(spot, XZ + dz)
+            self.go(spot, spot, XY + dz, "shard", p.beside)
+            self.go(spot, spot, XX + dz, "rep", p.across)
+            spot = self.whole.at[p.block(dz, 0), p.x, :, self.right]
+            self.came(spot, YZ + dz)
+            self.go(spot, spot, YX + dz, "rep", p.across)
+
+    def stage_third(self):
+        p = self.p
+        for dz in range(4):
+            spot = self.whole.at[p.block(dz, 1), p.x, :, self.left]
+            self.came(spot, XY + dz)
+            self.go(spot, spot, XX + 4 + dz, "rep", p.across)
+            if dz:
+                self.came(self.whole.at[p.block(dz, 0), 1 - p.x, :, self.right], YX + dz)
+                spot = self.whole.at[p.block(dz, 0), :, :, self.right]
+                self.go(spot, spot, YY + dz, "shard", p.beside)
+
+    def stage_core(self):
+        p = self.p
+        for dy in (0, 1):
+            for dz in range(4):
+                if dy or dz:
+                    self.came(self.whole.at[p.block(dz, dy), 1 - p.x, :, self.left], XX + 4 * dy + dz)
+                    if dy:
+                        self.came(self.whole.at[p.block(dz, 1), :, :, self.right], YY + dz)
+                    spot = self.whole.at[p.block(dz, dy), :, :, self.mine]
+                    self.go(spot, spot, CC + 4 * dy + dz, "rep", p.sibling)
+
+    def finish(self):
+        p = self.p
+        self.own_copy.wait()
+        for dy in (0, 1):
+            for dz in range(4):
+                if dy or dz:
+                    self.came(self.whole.at[p.block(dz, dy), :, :, self.theirs], CC + 4 * dy + dz)
+
+    def drain(self):
+        for shape, sem in self.started:
+            spot = self.whole.at[0, 0] if len(shape) == 2 else self.whole.at[0]
+            spot = spot.at[..., : shape[-1]]
+            rcopy(spot, spot, self.send.at[sem], self.recv.at[sem], "rep", self.p.sibling).wait_send()
+
+
 def one_hot(perm_ref, h, pt_ref):
     length = pt_ref.shape[0]
     row = perm_ref[pl.ds(h, 1), :].astype(jnp.int16)
@@ -57,14 +165,13 @@
     pt_ref[...] = jnp.where(places == row, jnp.ones((), BF16), jnp.zeros((), BF16))
 
 
-def fwd_kernel(
-    heads,
-    x_hbm, w_in_hbm, w_out_hbm, w_inner_hbm, w_outer_hbm, vec_ref, seg_ref, ok_ref, qperm_ref, kperm_ref, cot_hbm,
-    hid_hbm, act_hbm, din_hbm, flow_hbm, dou_hbm, dfi_hbm, dbr_hbm, att_hbm, head_hbm, xt_hbm, vgrad_ref,
-    xv, cot, w_in, w_out, w_inner, w_outer, qkv, qcode, kcode, ptq, ptk, att, head, xt,
-    act, din, flow, dou, dfi, dbr, hid, gp, fo, nf, ds,
-    in_sem, out_sem, head_sem,
-):
+def fwd_kernel(heads, remote, *refs):
+    (x_hbm, w_in_hbm, w_out_hbm, w_inner_hbm, w_outer_hbm, vec_ref, seg_ref, ok_ref, qperm_ref, kperm_ref, cot_hbm), refs = refs[:11], refs[11:]
+    (hid_hbm, act_hbm, din_hbm, flow_hbm, dou_hbm, dfi_hbm, dbr_hbm, att_hbm, head_hbm, xt_hbm, vgrad_ref), refs = refs[:11], refs[11:]
+    if remote:
+        (w_in_whole, w_out_whole), refs = refs[:2], refs[2:]
+    (xv, cot, w_in, w_out, w_inner, w_outer, qkv, qcode, kcode, ptq, ptk, att, head, xt), refs = refs[:14], refs[14:]
+    (act, din, flow, dou, dfi, dbr, hid, gp, fo, nf, ds, in_sem, out_sem, head_sem), refs = refs[:14], refs[14:]
     length, width = xv.shape
     hd = width // heads
     ff = act.shape[-1]
@@ -72,16 +179,45 @@
     fc = width
     n_in = 3 * width
 
-    loads = [
-        pltpu.make_async_copy(s, d, in_sem.at[i])
-        for i, (s, d) in enumerate(
-            ((x_hbm, xv), (w_in_hbm, w_in), (w_out_hbm, w_out), (w_inner_hbm, w_inner), (w_outer_hbm, w_outer), (cot_hbm, cot))
-        )
-    ]
-    for load in loads:
-        load.start()
-    vec = vec_ref[...].astype(F32)
-    vec_t = vec.T
+    if remote:
+        vslots, send, recv, vsend, vrecv, whole_sem = refs
+        p = Place()
+        barrier = pltpu.get_barrier_semaphore()
+        n_shard = lax.axis_size("shard")
+        for d in range(1, n_shard):
+            pl.semaphore_signal(barrier, inc=1, device_id={"shard": (p.shard + d) % n_shard}, device_id_type=pl.DeviceIdType.MESH)
+        for other in (p.sibling, p.across):
+            pl.semaphore_signal(barrier, inc=1, device_id={"rep": other}, device_id_type=pl.DeviceIdType.MESH)
+        weights = [
+            Gather(p, source, whole, split, send.at[a], recv.at[a])
+            for a, (source, whole, split) in enumerate(
+                ((w_in_hbm, w_in, 640), (w_out_hbm, w_out, 256), (w_inner_hbm, w_inner, 768), (w_outer_hbm, w_outer, 128))
+            )
+        ]
+        g_in, g_out, g_inner, g_outer = weights
+        pl.semaphore_wait(barrier, n_shard + 1)
+        g_in.stage_z()
+        shorts = [
+            rcopy(vec_ref, vslots.at[n_shard - d], vsend.at[n_shard - d], vrecv.at[n_shard - d], "shard", (p.shard + d) % n_shard)
+            for d in range(1, n_shard)
+        ]
+        for copy in shorts:
+            copy.start()
+        g_out.stage_z()
+        loads = [pltpu.make_async_copy(s, d, in_sem.at[i]) for i, (s, d) in enumerate(((x_hbm, xv), (cot_hbm, cot)))]
+        loads[0].start()
+        for weight in weights:
+            weight.own()
+        loads[1].start()
+    else:
+        loads = [
+            pltpu.make_async_copy(s, d, in_sem.at[i])
+            for i, (s, d) in enumerate(
+                ((x_hbm, xv), (w_in_hbm, w_in), (w_out_hbm, w_out), (w_inner_hbm, w_inner), (w_outer_hbm, w_outer), (cot_hbm, cot))
+            )
+        ]
+        for load in loads:
+            load.start()
 
     code_rows = lax.broadcasted_iota(jnp.int32, (16, length), 0)
     seg = seg_ref[...]
@@ -91,7 +227,25 @@
 
     loads[0].wait()
     xt[...] = xv[...].T
-    loads[1].wait()
+    if remote:
+        g_in.stage_second()
+        g_out.stage_second()
+        g_in.stage_third()
+        g_inner.stage_z()
+        g_in.stage_core()
+        g_out.stage_third()
+        for copy in shorts:
+            copy.wait_recv()
+        vec = vec_ref[...].astype(F32)
+        for d in range(1, n_shard):
+            vec = vec + vslots[d].astype(F32)
+        g_in.finish()
+        whole_in = pltpu.make_async_copy(w_in, w_in_whole, whole_sem.at[0])
+        whole_in.start()
+    else:
+        vec = vec_ref[...].astype(F32)
+        loads[1].wait()
+    vec_t = vec.T
     nt = 256
     for i in range(n_in // nt):
         n0 = i * nt
@@ -128,9 +282,24 @@
         combined = jnp.concatenate([mm(v_arr[:, c], probs[:, c], NN) for c in cols], axis=1)
         att[rows, :] = mm(combined.astype(BF16), ptq[...], NT).astype(BF16)
 
+    if remote:
+        g_out.stage_core()
+        g_outer.stage_z()
+        g_inner.stage_second()
+
     @pl.loop(0, heads)
     def _(h):
         attend(h)
+        if remote:
+            @pl.when(h == heads // 3)
+            def _():
+                g_inner.stage_third()
+                g_outer.stage_second()
+
+            @pl.when(h == 2 * heads // 3)
+            def _():
+                g_inner.stage_core()
+                g_outer.stage_third()
 
     heads_out = [
         pltpu.make_async_copy(s, d, head_sem.at[i])
@@ -138,8 +307,17 @@
     ]
     for copy in heads_out:
         copy.start()
-    for load in loads[2:]:
-        load.wait()
+    if remote:
+        g_outer.stage_core()
+        loads[1].wait()
+        g_out.finish()
+        whole_out = pltpu.make_async_copy(w_out, w_out_whole, whole_sem.at[1])
+        whole_out.start()
+        g_inner.finish()
+        g_outer.finish()
+    else:
+        for load in loads[2:]:
+            load.wait()
 
     b_out, g_first, s_first = vec[2:3, :], vec[3:4, :], vec[4:5, :]
     b_outer, g_second, s_second = vec[5:6, :], vec[6:7, :], vec[7:8, :]
@@ -224,13 +402,21 @@
             copy.wait()
     for copy in heads_out:
         copy.wait()
-
-
-def fwd_call(x, w_in, w_out, w_inner, w_outer, vec, seg, ok, qperm, kperm, cot):
+    if remote:
+        for weight in weights:
+            weight.drain()
+        for copy in shorts:
+            copy.wait_send()
+        whole_in.wait()
+        whole_out.wait()
+
+
+def fwd_call(remote, x, w_in, w_out, w_inner, w_outer, vec, seg, ok, qperm, kperm, cot):
     length, width = x.shape
     heads = qperm.shape[0]
     hd = width // heads
     ff = w_inner.shape[-1]
+    wholes = [(8, 2, w.shape[-2], w.shape[-1]) for w in (w_in, w_out, w_inner, w_outer)]
     tm = 256
     hbm = pl.BlockSpec(memory_space=pl.ANY)
     vmem = pl.BlockSpec(memory_space=pltpu.VMEM)
@@ -239,21 +425,31 @@
         ((length, width), F32), ((length, width), BF16), ((width, length), BF16), ((heads, 3 * hd + CL, length), BF16),
         ((width, length), BF16), ((16, width), F32),
     ]
+    if remote:
+        outs += [(wholes[0], BF16), (wholes[1], BF16)]
     scratch = [
-        ((length, width), BF16), ((length, width), BF16), (w_in.shape, BF16), (w_out.shape, BF16), (w_inner.shape, BF16), (w_outer.shape, BF16),
+        ((length, width), BF16), ((length, width), BF16), *[(whole, BF16) for whole in wholes],
         ((3 * width, length), BF16), ((16, length), BF16), ((16, length), BF16), ((length, length), BF16), ((length, length), BF16),
         ((width, length), BF16), ((heads, 3 * hd + CL, length), BF16), ((width, length), BF16),
         ((2, tm, ff), BF16), ((2, tm, ff), BF16), ((2, tm, width), BF16), ((2, tm, width), BF16), ((2, tm, width), F32), ((2, tm, width), BF16),
         ((2, tm, width), BF16), ((tm, ff), F32), ((tm, width), F32), ((tm, width), F32), ((tm, width), F32),
     ]
+    sems = [(6,), (2, 7), (3,)]
+    if remote:
+        n_shard = lax.axis_size("shard")
+        extra = [pltpu.VMEM((n_shard, 16, width), BF16)]
+        extra += [pltpu.SemaphoreType.DMA(n) for n in ((4, GATHER_SEMS), (4, GATHER_SEMS), (n_shard,), (n_shard,), (2,))]
+    else:
+        extra = []
     return pl.pallas_call(
-        partial(fwd_kernel, heads),
+        partial(fwd_kernel, heads, remote),
         out_shape=[jax.ShapeDtypeStruct(s, d) for s, d in outs],
         in_specs=[hbm] * 5 + [vmem] * 5 + [hbm],
-        out_specs=[hbm] * 10 + [vmem],
+        out_specs=[hbm] * 10 + [vmem] + [hbm] * (len(outs) - 11),
         scratch_shapes=[pltpu.VMEM(s, d) for s, d in scratch]
-        + [pltpu.SemaphoreType.DMA((6,)), pltpu.SemaphoreType.DMA((2, 7)), pltpu.SemaphoreType.DMA((3,))],
-        compiler_params=pltpu.CompilerParams(vmem_limit_bytes=60 << 20),
+        + [pltpu.SemaphoreType.DMA(n) for n in sems]
+        + extra,
+        compiler_params=pltpu.CompilerParams(vmem_limit_bytes=60 << 20, collective_id=0 if remote else None, has_side_effects=remote),
         name="layer_forward",
     )(x, w_in, w_out, w_inner, w_outer, vec, seg, ok, qperm, kperm, cot)
 
@@ -435,26 +631,41 @@
     n_shard = lax.axis_size("shard")
     shard = lax.axis_index("shard")
 
+    piece = width // n_shard
+    remote = n_shard == 8 and lax.axis_size("rep") == 4
+
     def whole(rows):
         return lax.all_gather(rows, "shard", axis=0, tiled=True)
 
     def blocked(rows):
         return rows.reshape(8, 2, rows.shape[0] // 16, rows.shape[1])
 
-    w_in, w_out, w_inner, w_outer = [blocked(whole(w)) for w in (in_weight, out_weight, inner_weight, outer_weight)]
+    def halved(rows):
+        return rows.reshape(2, rows.shape[0] // 2, rows.shape[1])
+
+    weights = (in_weight, out_weight, inner_weight, outer_weight)
     short = jnp.stack([query_bias, value_bias, out_bias, first_gain, first_shift, outer_bias, second_gain, second_shift])
-    vectors = lax.all_gather(jnp.concatenate([short.reshape(-1), inner_bias]), "shard", axis=0)
-    piece = width // n_shard
-    vec = jnp.concatenate(
-        [
-            jnp.transpose(vectors[:, : 8 * piece].reshape(n_shard, 8, piece), (1, 0, 2)).reshape(8, width),
-            vectors[:, 8 * piece :].reshape(ff // width, width),
-            jnp.zeros((8 - ff // width, width), BF16),
-        ]
+    inner_piece = ff // n_shard
+    if remote:
+        w_in, w_out, w_inner, w_outer = [halved(w) for w in weights]
+        vec = lax.dynamic_update_slice(jnp.zeros((16, width), BF16), short, (0, shard * piece))
+        first = shard * inner_piece
+        vec = lax.dynamic_update_slice(vec, inner_bias[None], (8 + first // width, first % width))
+    else:
+        w_in, w_out, w_inner, w_outer = [blocked(whole(w)) for w in weights]
+        vectors = lax.all_gather(jnp.concatenate([short.reshape(-1), inner_bias]), "shard", axis=0)
+        vec = jnp.concatenate(
+            [
+                jnp.transpose(vectors[:, : 8 * piece].reshape(n_shard, 8, piece), (1, 0, 2)).reshape(8, width),
+                vectors[:, 8 * piece :].reshape(ff // width, width),
+                jnp.zeros((8 - ff // width, width), BF16),
+            ]
+        )
+    hidden, act, din, flow, dou, dfi, dbr, att, head, xt, vg, *wholes = fwd_call(
+        remote, layer_input[0], w_in, w_out, w_inner, w_outer, vec, segment_ids, token_valid, query_perm[0], key_perm[0], out_cotangent[0]
     )
-    hidden, act, din, flow, dou, dfi, dbr, att, head, xt, vg = fwd_call(
-        layer_input[0], w_in, w_out, w_inner, w_outer, vec, segment_ids, token_valid, query_perm[0], key_perm[0], out_cotangent[0]
-    )
+    if remote:
+        w_in, w_out = wholes
     grad_x, g_in, g_out, g_inner, g_outer, vg = bwd_call(
         act, din, flow, dou, dfi, dbr, att, head, xt, w_in, w_out, query_perm[0], key_perm[0], vg
     )
@@ -469,7 +680,6 @@
     d_in, d_out, d_inner, d_outer = [summed(g) for g in grads]
     vg = lax.psum(vg, ("rep", "shard"))
     mine = lax.dynamic_slice(vg, (0, shard * piece), (8, piece))
-    inner_piece = ff // n_shard
     inner_mine = lax.dynamic_slice(vg[8 : 8 + ff // width].reshape(ff), (shard * inner_piece,), (inner_piece,))
     return (
         hidden[None], grad_x[None], d_in, mine[0], mine[1], d_out, mine[2], mine[3], mine[4], d_inner, inner_mine, d_outer,

time: 1030 us -> 822 us (0.80)
  waiting for transfers between devices: 732 us -> 498 us
  Pallas kernels: 142 us -> 197 us
  blocking collectives: 72.7 us -> 40.2 us
    all_gather x4 -> x0, waiting for transfers between devices: 234 us -> none  [whole(): return lax.all_gather(rows, 'shard', axis=0, tiled=True)]
    pallas_call x1, Pallas kernels: 69 us -> 124 us  [fwd_call(): pl.pallas_call(partial(fwd_kernel, heads, remote), out_shape=[jax.ShapeDt...]
    all_gather x1 -> x0, blocking collectives: 32.4 us -> none  [shards(): lax.all_gather(jnp.concatenate([short.reshape(-1), inner_bias]), 'shard',...]
    unnamed x10 -> x6, waiting for transfers between devices: 133 us -> 130 us
  transfers between devices with their start and end apart: 9 -> 5, of which waited for: 9 -> 5; matrix products, arithmetic and copies ran while one was open for 5% -> 6% of each run, Pallas kernels for 0% -> 0%
where the time goes in v2:
time: 822 us; the launch traced here: 816 us
  waiting for transfers between devices  498 us (61%)
  Pallas kernels  197 us (24%)
  blocking collectives  40.2 us (5%)
  local copies, waits for them, and re-layouts  37.7 us (5%)
  other arithmetic  27.9 us (3%)
  between operations  14.1 us (2%)
    reduce_scatter x3, waiting for transfers between devices, summed(): lax.psum_scatter(grad.astype(F32), 'shard', scatter_dimension=0, tiled=True)  359 us
    unnamed x6, waiting for transfers between devices  130 us
    pallas_call x1, Pallas kernels, fwd_call(): pl.pallas_call(partial(fwd_kernel, heads, remote), out_shape=[jax.ShapeDt...  124 us
    pallas_call x1, Pallas kernels, bwd_call(): pl.pallas_call(partial(bwd_kernel, heads), out_shape=[jax.ShapeDtypeStruc...  73.4 us
    psum x1, blocking collectives, shards(): vg = lax.psum(vg, ('rep', 'shard'))  40.2 us
    convert_element_type x2, local copies, waits for them, and re-layouts, summed(): grad.astype(F32)  18.5 us
    convert_element_type x3, other arithmetic, summed(): grad.astype(F32)  16.9 us
  transfers between devices with their start and end apart: 5, of which 5 were waited for; matrix products, arithmetic and copies ran while one was open for 6% of the time, Pallas kernels for 0%

profile of v2, /device:TPU:0, one launch (start us, length us, event | category | flops | bytes accessed | tf_op | source)
XLA Modules:
  0.0 815.8 jit_solution(5487474903624152267)
XLA Ops:
  7.3 0.7 broadcast_in_dim.13
  7.9 1.5 copy_bitcast_fusion
  9.4 0.8 stack.35
  10.2 0.3 dynamic_update_slice.6
  10.6 0.3 dynamic_update_slice.7.refs_5_
  10.8 0.6 copy-done.3
  11.4 124.0 %layer_forward.1 = (bf16[1024,768]{1,0:T(8,128)(2,1)}, bf16[1024,3072]{1,0:T(8,128)(2,1)}, bf16[1024,3072]{1,0:T(8,128)(2,1)}, bf16[1024,768]{1,0:T(8,128)(2,1)}...) custom-call(bf16[1024,768]{1,0:T(8,128)(2,1)} %bitcast.52, ...), custom_call_target="tpu_custom_call" | custom-call | tf_op jit(solution)/shard_map/layer_forward/pallas_call | solution.py:444
  135.5 73.4 %layer_backward.1 = (bf16[1024,768]{1,0:T(8,128)(2,1)}, bf16[3,8,2,48,768]{4,3,2,1,0:T(8,128)(2,1)}, bf16[8,2,48,768]{3,2,1,0:T(8,128)(2,1)}, bf16[8,2,48,3072]{...) custom-call(bf16[1024,3072]{1,0:T(8,128)(2,1)} %get-tuple-element.35.act_hbm, ...), custom_call_target="tpu_custom_call" | custom-call | tf_op jit(solution)/shard_map/layer_backward/pallas_call | solution.py:612
  208.9 3.0 bitcast_convert_fusion.2
  211.9 7.7 reshape.69
  219.6 10.8 %copy.37 = f32[768,3,3,256]{0,3,2,1:T(8,128)} copy(f32[768,3,3,256]{3,1,0,2:T(4,128)} %bitcast.50) | data formatting | bytes 14155776 | tf_op jit(solution)/shard_map/convert_element_type | solution.py:677
  230.4 8.1 copy.39
  238.6 7.2 bitcast_convert_fusion.1
  245.9 6.8 bitcast_convert_fusion
  252.7 30.4 %reduce-scatter.7.cloned.1.call-done = f32[96,768]{1,0:T(8,128)} async-done(((f32[768,768]{1,0:T(8,128)}), f32[96,768]{1,0:T(8,128)}) %reduce-scatter.7.cloned.1.call-update) | async-done | bytes 294928 | tf_op jit(solution)/shard_map/reduce_scatter | solution.py:677
  283.1 1.6 convert_element_type.62
  284.7 130.2 %reduce-scatter.13.cloned.1.call-done = f32[96,2304]{1,0:T(8,128)} async-done(((f32[768,2304]{1,0:T(8,128)}), f32[96,2304]{1,0:T(8,128)}) %reduce-scatter.13.cloned.1.call-update) | async-done | bytes 884752
  414.9 2.2 copy.40
  417.1 164.2 %reduce-scatter.9.cloned.1.call-done = f32[96,3072]{1,0:T(8,128)} async-done(((f32[768,3072]{1,0:T(8,128)}), f32[96,3072]{1,0:T(8,128)}) %reduce-scatter.9.cloned.1.call-update) | async-done | bytes 1179664 | tf_op jit(solution)/shard_map/reduce_scatter | solution.py:677
  581.3 2.2 convert_element_type.66
  583.5 164.2 %reduce-scatter.11.cloned.1.call-done = f32[384,768]{1,0:T(8,128)} async-done(((f32[3072,768]{1,0:T(8,128)}), f32[384,768]{1,0:T(8,128)}) %reduce-scatter.11.cloned.1.call-update) | async-done | bytes 1179664 | tf_op jit(solution)/shard_map/reduce_scatter | solution.py:677
  747.6 2.1 convert_element_type.70
  749.8 40.2 %psum.36 = f32[16,768]{1,0:T(8,128)S(1)} all-reduce(f32[16,768]{1,0:T(8,128)S(1)} %copy-done.4), channel_id=1, replica_groups=mesh['rep'=4,'shard'=8] {'rep','shard'}, use_global_device_ids=true, to_apply=%region_2.3 | all-reduce | flops 12288 | bytes 98304 | tf_op jit(solution)/shard_map/psum | solution.py:681
  790.0 0.7 dynamic_slice.7
  790.7 0.1 constant_dynamic-slice_fusion
  790.8 0.5 slice_bitcast_fusion
  791.3 9.3 %all-reduce.3.cloned.1.call-done = (bf16[96,2304]{0,1:T(8,128)(2,1)}, bf16[96,768]{1,0:T(8,128)(2,1)}, bf16[96,3072]{1,0:T(8,128)(2,1)}, bf16[384,768]{1,0:T(8,128)(2,1)}) async-done(((bf16[96,2304]{0,1:T(8,128)(2,1)}, bf16[96,768]{1,0:T(8,128)(2,1)}, bf16[96,3072]{1,0:T(8,128)(2,1)}, bf16[384,768]{1,0:T(8,128)(2,1)}), (bf16[96,2304]{0,1:T(8,128)(2,1)}, bf16[96,768]{1,0:T(8,128)(2,1)}, ...) | async-done | bytes 1769488 | tf_op jit(solution)/shard_map/psum | solution.py:678
  800.6 2.3 copy.38
  802.9 1.8 convert_element_type.63
  804.7 2.2 convert_element_type.67
  806.9 1.1 convert_element_type.71
  807.9 1.1 copy.52
  (22 shorter events, 0.3 us)
Async XLA Ops:
  7.2 275.9 %reduce-scatter.7.cloned.1.call-start = ((), (), s32[]{:S(2)}) async-start(), calls=%async_computation.4 | async-start | bytes 2654208 | tf_op jit(solution)/shard_map/reduce_scatter | solution.py:677
  10.8 0.6 copy-start.3
  208.8 3.1 copy-start
  211.9 203.0 %reduce-scatter.13.cloned.1.call-start = ((), (), s32[]{:S(2)}) async-start(), calls=%async_computation.7 | async-start | bytes 7962624
  238.5 342.8 %reduce-scatter.9.cloned.1.call-start = ((), (), s32[]{:S(2)}) async-start(), calls=%async_computation.5 | async-start | bytes 10616832 | tf_op jit(solution)/shard_map/reduce_scatter | solution.py:677
  245.8 501.8 %reduce-scatter.11.cloned.1.call-start = ((), (), s32[]{:S(2)}) async-start(), calls=%async_computation.6 | async-start | bytes 10616832 | tf_op jit(solution)/shard_map/reduce_scatter | solution.py:677
  252.6 548.0 %all-reduce.3.cloned.1.call-start = ((), (), s32[]{:S(2)}) async-start(), calls=%async_computation.8 | async-start | bytes 3833856 | tf_op jit(solution)/shard_map/psum | solution.py:678
  417.1 332.7 %copy-start.4 = (f32[16,768]{1,0:T(8,128)S(1)}, f32[16,768]{1,0:T(8,128)}, u32[]{:S(2)}) copy-start(f32[16,768]{1,0:T(8,128)} %get-tuple-element.49) | copy-start | bytes 147460
  800.6 6.2 copy-start.2
  802.9 5.0 copy-start.1
Sparse Core Ops, SparseCore 0:
  212.0 71.0 reduce-scatter.6
  286.8 128.0 reduce-scatter.12
  418.9 162.3 reduce-scatter.8
  585.2 162.3 reduce-scatter.10
  751.4 49.1 all-reduce.2

commit v3 on v1

v3 whole, which is shorter than its diff:
```python
from functools import partial

import jax
import jax.numpy as jnp
from jax import lax
from jax.experimental import pallas as pl
from jax.experimental.pallas import tpu as pltpu
from jax.sharding import PartitionSpec as P

CL = 128
EPS = 1e-06
BIG = 2.0**100
F32 = jnp.float32
BF16 = jnp.bfloat16
NN = (((1,), (0,)), ((), ()))
NT = (((1,), (1,)), ((), ()))
TN = (((0,), (0,)), ((), ()))
TT = (((0,), (1,)), ((), ()))


def mm(a, b, dims):
    return lax.dot_general(a, b, dims, preferred_element_type=F32)


def rows2(value):
    return value.reshape(value.shape[0] * value.shape[1] * value.shape[2], value.shape[3])


def norm_parts(resid):
    average = jnp.mean(resid, axis=-1, keepdims=True)
    centred = resid - average
    variance = jnp.mean(centred * centred, axis=-1, keepdims=True)
    inv_std = lax.rsqrt(variance + EPS)
    return centred * inv_std, inv_std


def norm_back(grad_out, normed, inv_std, gain):
    scaled = grad_out * gain
    first_term = jnp.mean(scaled, axis=-1, keepdims=True)
    second_term = jnp.mean(scaled * normed, axis=-1, keepdims=True)
    return inv_std * (scaled - first_term - normed * second_term)


def gelu_both(z):
    gauss = jnp.exp(-0.5 * (z * z))
    t = 1.0 / (1.0 + (0.3275911 * 0.7071067811865476) * jnp.abs(z))
    poly = t * (0.127414796 + t * (-0.142248368 + t * (0.7107068705 + t * (-0.7265760135 + t * 0.5307027145))))
    tail = poly * gauss
    phi = jnp.where(z >= 0.0, 1.0 - tail, tail)
    return z * phi, phi + z * gauss * 0.3989422804014327


def rcopy(src, dst, send, recv, axis, index):
    return pltpu.make_async_remote_copy(
        src_ref=src, dst_ref=dst, send_sem=send, recv_sem=recv, device_id={axis: index}, device_id_type=pl.DeviceIdType.MESH
    )


class Place:
    def __init__(self):
        rep, shard = lax.axis_index("rep"), lax.axis_index("shard")
        self.x, self.c = rep // 2, rep % 2
        self.z, self.y = shard // 2, shard % 2
        self.rep, self.shard = rep, shard
        self.sibling = self.x * 2 + (1 - self.c)
        self.across = (1 - self.x) * 2 + self.c
        self.beside = self.z * 2 + (1 - self.y)

    def plane(self, dz):
        return (self.z + dz) % 4

    def block(self, dz, dy):
        return self.plane(dz) * 2 + (self.y + dy) % 2


GZ, GX, GA, GB, GC, GD, GATHER_SEMS = 0, 3, 6, 7, 8, 11, 12


class Gather:
    def __init__(self, place, whole, rows, start, size, kind, send, recv):
        half = whole.shape[-1] // 2
        self.p, self.rows, self.size, self.kind, self.send, self.recv = place, rows, size, kind, send, recv
        self.whole = whole.reshape(4, 2, 2, *whole.shape[2:])
        self.mine = pl.ds(pl.multiple_of(place.c * half + start, 128), size)
        self.theirs = pl.ds(pl.multiple_of((1 - place.c) * half + start, 128), size)

    def spot(self, z, y, x, columns=None):
        return self.whole.at[z, y, x, self.rows, self.mine if columns is None else columns]

    def go(self, spot, sem, axis, index):
        rcopy(spot, spot, self.send.at[sem], self.recv.at[sem], axis, index).start()

    def came(self, spot, sem):
        rcopy(spot, spot, self.send.at[sem], self.recv.at[sem], "rep", self.p.sibling).wait_recv()

    def first(self):
        p = self.p
        for dz in (1, 2, 3):
            self.go(self.spot(p.z, p.y, p.x), GZ + 3 - dz, "shard", p.plane(dz) * 2 + p.y)

    def second(self):
        p = self.p
        for dz in (1, 2, 3):
            spot = self.spot(p.plane(dz), p.y, p.x)
            self.came(spot, GZ + dz - 1)
            self.go(spot, GX + dz - 1, "rep", p.across)
        if self.kind == "x":
            self.go(self.spot(slice(None), p.y, p.x), GA, "shard", p.beside)

    def third(self):
        p = self.p
        if self.kind == "x":
            spot = self.spot(slice(None), 1 - p.y, p.x)
            self.came(spot, GA)
            self.go(spot, GB, "rep", p.across)
        for dz in (1, 2, 3):
            self.came(self.spot(p.plane(dz), p.y, 1 - p.x), GX + dz - 1)
        if self.kind == "y":
            self.go(self.spot(slice(None), p.y, slice(None)), GA, "shard", p.beside)
        for dz in (1, 2, 3):
            self.go(self.spot(p.plane(dz), p.y, slice(None)), GC + dz - 1, "rep", p.sibling)

    def fourth(self):
        p = self.p
        if self.kind == "x":
            self.came(self.spot(slice(None), 1 - p.y, 1 - p.x), GB)
        else:
            self.came(self.spot(slice(None), 1 - p.y, slice(None)), GA)
        self.go(self.spot(slice(None), 1 - p.y, slice(None)), GD, "rep", p.sibling)

    def last(self):
        p = self.p
        for dz in (1, 2, 3):
            self.came(self.spot(p.plane(dz), p.y, slice(None), self.theirs), GC + dz - 1)
        self.came(self.spot(slice(None), 1 - p.y, slice(None), self.theirs), GD)

    def drain(self):
        every = slice(None)
        columns = slice(0, self.size)
        one, four, pair, eight = (0, 0, 0), (every, 0, 0), (0, 0, every), (every, 0, every)
        sizes = {GA: four if self.kind == "x" else eight, GB: four, GD: eight}
        for dz in range(3):
            sizes.update({GZ + dz: one, GX + dz: one, GC + dz: pair})
        if self.kind == "y":
            del sizes[GB]
        for sem, (z, y, x) in sizes.items():
            spot = self.spot(z, y, x, columns)
            rcopy(spot, spot, self.send.at[sem], self.recv.at[sem], "rep", self.p.sibling).wait_send()


SC, S1, S2, SZ, SX, SL, SCATTER_SEMS = 0, 1, 2, 3, 6, 7, 8


def scatter_buffers(rows, size):
    return [(4, 2, 2, rows, size), (4, 2, rows, size), (4, rows, size), (3, rows, size)]


class Scatter:
    def __init__(self, place, part, out, rows, start, size, kind, buffers, send, recv):
        half = part.shape[-1] // 2
        self.p, self.kind, self.send, self.recv, self.out, self.rows, self.size = place, kind, send, recv, out, rows, size
        self.part = part.reshape(4, 2, 2, *part.shape[2:])
        self.one, self.two, self.three, self.four = buffers
        self.mine = pl.ds(pl.multiple_of(place.c * half + start, 128), size)
        self.theirs = pl.ds(pl.multiple_of((1 - place.c) * half + start, 128), size)

    def go(self, src, dst, sem, axis, index):
        rcopy(src, dst, self.send.at[sem], self.recv.at[sem], axis, index).start()

    def came(self, dst, sem):
        rcopy(dst, dst, self.send.at[sem], self.recv.at[sem], "rep", self.p.sibling).wait_recv()

    def core(self):
        self.go(self.part.at[:, :, :, self.rows, self.theirs], self.one, SC, "rep", self.p.sibling)

    def first(self):
        p = self.p
        self.came(self.one, SC)

        @pl.loop(0, 4)
        def _(z):
            self.one[z] = self.one[z] + self.part[z, :, :, self.rows, self.mine]

        if self.kind == "x":
            self.go(self.one.at[:, :, 1 - p.x], self.two, S1, "rep", p.across)
        else:
            self.go(self.one.at[:, 1 - p.y], self.two, S1, "shard", p.beside)

    def second(self):
        p = self.p
        self.came(self.two, S1)
        if self.kind == "x":
            self.two[...] = self.two[...] + self.one[:, :, p.x]
            self.go(self.two.at[:, 1 - p.y], self.three, S2, "shard", p.beside)
        else:
            self.two[...] = self.two[...] + self.one[:, p.y]
            self.go(self.two.at[:, 1 - p.x], self.three, S2, "rep", p.across)

    def third(self):
        p = self.p
        self.came(self.three, S2)
        self.three[...] = self.three[...] + self.two[:, p.y if self.kind == "x" else p.x]
        for dz in (1, 2, 3):
            self.go(self.three.at[p.plane(dz)], self.four.at[3 - dz], SZ + 3 - dz, "shard", p.plane(dz) * 2 + p.y)

    def fourth(self):
        p = self.p
        total = self.three[p.z].astype(F32)
        for dz in range(3):
            self.came(self.four.at[dz], SZ + dz)
            total = total + self.four[dz].astype(F32)
        self.out[p.x, self.rows, self.mine] = total.astype(BF16)
        spot = self.out.at[p.x, self.rows, self.mine]
        self.go(spot, spot, SX, "rep", p.across)

    def fifth(self):
        p = self.p
        self.came(self.out.at[1 - p.x, self.rows, self.mine], SX)
        spot = self.out.at[:, self.rows, self.mine]
        self.go(spot, spot, SL, "rep", p.sibling)

    def last(self):
        self.came(self.out.at[:, self.rows, self.theirs], SL)

    def drain(self):
        columns = slice(0, self.size)
        spots = [(self.one, SC), (self.two, S1), (self.three, S2)] + [(self.four.at[dz], SZ + dz) for dz in range(3)]
        spots += [(self.out.at[0, self.rows, columns], SX), (self.out.at[:, self.rows, columns], SL)]
        for spot, sem in spots:
            rcopy(spot, spot, self.send.at[sem], self.recv.at[sem], "rep", self.p.sibling).wait_send()


def one_hot(perm_ref, h, pt_ref):
    length = pt_ref.shape[0]
    row = perm_ref[pl.ds(h, 1), :].astype(jnp.int16)
    places = lax.broadcasted_iota(jnp.int16, (length, length), 0)
    pt_ref[...] = jnp.where(places == row, jnp.ones((), BF16), jnp.zeros((), BF16))


HG = 4

GATHERED = [("in0", 0, 0, 256, "x"), ("in0", 0, 256, 128, "y"), ("in1", 0, 0, 384, "x"), ("in2", 0, 0, 384, "y"), ("out", 0, 0, 384, "x")]
GATHERED += [("inner", 0, n * 384, 384, "yx"[n % 2]) for n in range(4)]
GATHERED += [("outer", n * 48, 0, 384, "xxyx"[n]) for n in range(4)]
IN0, IN1, IN2, OUT, INNER, OUTER = [0, 1], [2], [3], [4], [5, 6, 7, 8], [9, 10, 11, 12]
AT_START = [(1, 0), (1, 1)]
AHEAD = [(2, 0), (1, 2), (2, 1), (1, 3), (3, 0), (3, 1), (2, 2), (1, 4), (4, 0), (4, 1), (2, 3), (1, 5), (5, 0), (5, 1)]
AT_HEAD = {1: [(3, 2), (3, 3), (2, 4), (2, 5), (1, 6), (1, 7)], 3: [(4, 2), (2, 6), (1, 8)], 4: [(4, 3), (5, 2)], 5: [(3, 4), (3, 5), (2, 7), (2, 8), (1, 9), (1, 10)], 6: [(3, 6)], 7: [(4, 4), (2, 9), (1, 11)], 8: [(4, 5), (3, 7), (2, 10), (1, 12), (5, 3)], 9: [(4, 6), (3, 8), (2, 11)], 10: [(3, 9), (2, 12)]}
AT_FFN = [(5, 4), (5, 5), (5, 6), (4, 7), (5, 7), (4, 8), (5, 8)]
AT_TILE = {0: [(3, 10), (3, 11), (4, 9)], 1: [(4, 10), (3, 12)], 2: [(4, 11), (4, 12)]}
AT_BACK = [(5, 9), (5, 10), (5, 11), (5, 12)]
STAGES = ("", "first", "second", "third", "fourth", "last")


def fwd_kernel(heads, remote, *refs):
    (x_hbm, w_in_hbm, w_out_hbm, w_inner_hbm, w_outer_hbm, vec_ref, seg_ref, ok_ref, qperm_ref, kperm_ref, cot_hbm), refs = refs[:11], refs[11:]
    (hid_hbm, act_hbm, din_hbm, flow_hbm, dou_hbm, dfi_hbm, dbr_hbm, att_hbm, head_hbm, xt_hbm, vgrad_ref), refs = refs[:11], refs[11:]
    if remote:
        (w_in_whole, w_out_whole), refs = refs[:2], refs[2:]
    (xv, cot, w_in, w_out, w_inner, w_outer, qkv, vcol, qcode, kcode, ptq, ptk, att, head, xt), refs = refs[:15], refs[15:]
    (act, gp, flow, fo, nf, inv, dou, dfi, dbr, hid, ds, in_sem, act_sem, out_sem, head_sem, once_sem), refs = refs[:16], refs[16:]
    length, width = xv.shape
    hd = width // heads
    tm, ff = act.shape[1:]
    fc = width
    groups = heads // HG
    gw = HG * hd
    n_tiles = length // tm
    copy = pltpu.make_async_copy

    loads = {"x": copy(x_hbm, xv, in_sem.at[0]), "cot": copy(cot_hbm, cot, in_sem.at[1])}
    pairs = ((w_out_hbm, w_out), (w_inner_hbm, w_inner), (w_outer_hbm, w_outer))
    if remote:
        vslots, send, recv, vsend, vrecv, whole_sem = refs
        p = Place()
        n_shard = lax.axis_size("shard")
        owns = [
            copy(w_in_hbm.at[:, :, pl.ds(q * width + g * gw, gw)], w_in.at[g, p.shard, :, :, pl.ds(q * gw, gw)], in_sem.at[5 + 3 * g + q])
            for g in range(groups)
            for q in range(3)
        ]
        owns += [copy(source, whole.at[p.shard], in_sem.at[2 + n]) for n, (source, whole) in enumerate(pairs)]
        for own in owns:
            own.start()
        for name in ("x", "cot"):
            loads[name].start()
        barrier = pltpu.get_barrier_semaphore()
        for d in range(1, n_shard):
            pl.semaphore_signal(barrier, inc=1, device_id={"shard": (p.shard + d) % n_shard}, device_id_type=pl.DeviceIdType.MESH)
        for other in (p.sibling, p.across):
            pl.semaphore_signal(barrier, inc=1, device_id={"rep": other}, device_id_type=pl.DeviceIdType.MESH)
        wholes = {"in0": w_in.at[0], "in1": w_in.at[1], "in2": w_in.at[2], "out": w_out, "inner": w_inner, "outer": w_outer}
        units = [
            Gather(p, wholes[name], slice(row, row + 48), start, size, kind, send.at[u], recv.at[u])
            for u, (name, row, start, size, kind) in enumerate(GATHERED)
        ]
        shorts = [
            rcopy(vec_ref, vslots.at[n_shard - d], vsend.at[n_shard - d], vrecv.at[n_shard - d], "shard", (p.shard + d) % n_shard)
            for d in range(1, n_shard)
        ]

        def pump(steps):
            for stage, u in steps:
                getattr(units[u], STAGES[stage])()

        for own in owns:
            own.wait()
        pl.semaphore_wait(barrier, n_shard + 1)
        pump(AT_START)
        for short in shorts:
            short.start()
    else:
        owns = [copy(w_in_hbm, w_in, in_sem.at[5])] + [copy(source, whole, in_sem.at[2 + n]) for n, (source, whole) in enumerate(pairs)]
        for own in owns:
            own.start()
        for name in ("x", "cot"):
            loads[name].start()

        def pump(steps):
            pass

    code_rows = lax.broadcasted_iota(jnp.int32, (16, length), 0)
    seg = seg_ref[...]
    ok = ok_ref[...] > 0
    qcode[...] = jnp.where(code_rows == jnp.where(ok, seg, 4), 1.0, 0.0).astype(BF16)
    kcode[...] = jnp.where((code_rows < 5) & (code_rows != jnp.where(ok, seg, 5)), -BIG, 0.0).astype(BF16)
    vgrad_ref[...] = jnp.zeros_like(vgrad_ref)
    loads["x"].wait()
    xt[...] = xv[...].T
    xt_copy = copy(xt, xt_hbm, once_sem.at[0])
    xt_copy.start()
    vec = vec_ref[...].astype(F32)
    if remote:
        for short in shorts:
            short.wait_recv()
        for d in range(1, n_shard):
            vec = vec + vslots[d].astype(F32)
        pump(AHEAD)
    else:
        for own in owns:
            own.wait()
    vcol[...] = vec.T

    def head_copy(h, slot):
        return copy(head.at[slot], head_hbm.at[h], head_sem.at[slot])

    def project(g):
        for q in range(3):
            weight = rows2(w_in[g, :, :, :, q * gw : (q + 1) * gw])
            acc = mm(weight, xt[...], TN)
            bias = vcol[pl.ds(pl.multiple_of(g * gw, gw), gw), :]
            if q == 0:
                acc = (acc + bias[:, 0:1]).astype(BF16) * 0.125
            elif q == 2:
                acc = acc + bias[:, 1:2]
            qkv[q * gw : (q + 1) * gw, :] = acc.astype(BF16)

    def attend(h):
        slot = lax.rem(h, 2)
        r0 = pl.multiple_of(lax.rem(h, HG) * hd, hd)
        rows = pl.ds(pl.multiple_of(h * hd, hd), hd)
        one_hot(qperm_ref, h, ptq)
        one_hot(kperm_ref, h, ptk)
        q_side = jnp.concatenate([qkv[pl.ds(r0, hd), :], qcode[...]], axis=0)
        k_side = jnp.concatenate(
            [qkv[pl.ds(pl.multiple_of(gw + r0, hd), hd), :], kcode[...], qkv[pl.ds(pl.multiple_of(2 * gw + r0, hd), hd), :]], axis=0
        )
        q_arr = mm(q_side, ptq[...], NN).astype(BF16)
        k_arr = mm(k_side, ptk[...], NN).astype(BF16)
        v_arr = k_arr[hd + 16 :, :]

        @pl.when(h >= 2)
        def _():
            head_copy(h - 2, slot).wait()

        head[slot, :hd, :] = q_arr[:hd, :]
        head[slot, hd : 2 * hd, :] = k_arr[:hd, :]
        head[slot, 2 * hd : 3 * hd, :] = v_arr
        cols = [slice(c * CL, (c + 1) * CL) for c in range(length // CL)]
        scores = jnp.concatenate([mm(k_arr[: hd + 16, c], q_arr[:, c], TN) for c in cols], axis=1)
        top = jnp.maximum(jnp.max(scores, axis=0, keepdims=True), -1e29)
        raised = jnp.exp(scores - top)
        total = jnp.maximum(jnp.sum(raised, axis=0, keepdims=True), 1.0)
        probs = (raised * (1.0 / total)).astype(BF16)
        head[slot, 3 * hd :, :] = probs
        head_copy(h, slot).start()
        combined = jnp.concatenate([mm(v_arr[:, c], probs[:, c], NN) for c in cols], axis=1)
        att[rows, :] = mm(combined.astype(BF16), ptq[...], NT).astype(BF16)

    @pl.loop(0, heads)
    def _(h):
        for at in AT_HEAD if remote else ():
            @pl.when(h == at)
            def _():
                pump(AT_HEAD[at])

        @pl.when(lax.rem(h, HG) == 0)
        def _():
            project(h // HG)

        attend(h)

    att_copy = copy(att, att_hbm, once_sem.at[1])
    att_copy.start()
    if remote:
        pump(AT_FFN)
        whole_copies = [copy(w_in, w_in_whole, whole_sem.at[0]), copy(w_out, w_out_whole, whole_sem.at[1])]
        for one in whole_copies:
            one.start()
    b_out, g_first, s_first = vec[2:3, :], vec[3:4, :], vec[4:5, :]
    b_outer, g_second, s_second = vec[5:6, :], vec[6:7, :], vec[7:8, :]

    def add_row(row, value):
        vgrad_ref[row : row + 1, :] += jnp.sum(value, axis=0, keepdims=True)

    def row_copies(i, which):
        rows = pl.ds(pl.multiple_of(i * tm, tm), tm)
        if which == 0:
            return [copy(act.at[i], act_hbm.at[rows, :], act_sem.at[i, 0]), copy(flow.at[i], flow_hbm.at[rows, :], act_sem.at[i, 1])]
        if which == 1:
            return [copy(gp.at[i], din_hbm.at[rows, :], act_sem.at[i, 2])]
        slot = lax.rem(i, 2)
        return [
            copy(s.at[slot], d.at[rows, :], out_sem.at[slot, n])
            for n, (s, d) in enumerate(((dou, dou_hbm), (dfi, dfi_hbm), (dbr, dbr_hbm), (hid, hid_hbm)))
        ]

    @pl.loop(0, n_tiles)
    def _(i):
        for at in AT_TILE if remote else ():
            @pl.when(i == at)
            def _():
                pump(AT_TILE[at])

        rows = pl.ds(pl.multiple_of(i * tm, tm), tm)
        branch = mm(att[:, rows], rows2(w_out[...]), TN)
        normed, inv_first = norm_parts(xv[rows, :].astype(F32) + branch + b_out)
        nf[i] = normed
        inv[i] = inv_first
        first_out = normed * g_first + s_first
        fo[i] = first_out
        flow[i] = first_out.astype(BF16)
        for j in range(ff // fc):
            cols = slice(j * fc, (j + 1) * fc)
            inner = mm(flow[i], rows2(w_inner[:, :, :, cols]), NN) + vec[8 + j : 9 + j, :]
            high, slope = gelu_both(inner)
            act[i, :, cols] = high.astype(BF16)
            gp[i, :, cols] = slope.astype(BF16)
        for one in row_copies(i, 0):
            one.start()

    if remote:
        pump(AT_BACK)
    loads["cot"].wait()
    per = w_outer.shape[0] * fc // ff

    @pl.loop(0, n_tiles)
    def _(i):
        slot = lax.rem(i, 2)
        rows = pl.ds(pl.multiple_of(i * tm, tm), tm)

        @pl.when(i >= 2)
        def _():
            for one in row_copies(i - 2, 2):
                one.wait()

        outer = None
        for j in range(ff // fc):
            term = mm(act[i, :, j * fc : (j + 1) * fc], rows2(w_outer[j * per : (j + 1) * per]), NN)
            outer = term if outer is None else outer + term
        normed_second, inv_second = norm_parts(fo[i] + outer + b_outer)
        hid[slot] = (normed_second * g_second + s_second).astype(BF16)
        grad = cot[rows, :].astype(F32)
        d_second = norm_back(grad, normed_second, inv_second, g_second)
        add_row(6, grad * normed_second)
        add_row(7, grad)
        ds[...] = d_second
        low = d_second.astype(BF16)
        dou[slot] = low
        add_row(5, low.astype(F32))
        back = None
        for j in range(ff // fc):
            cols = slice(j * fc, (j + 1) * fc)
            d_act = mm(dou[slot], rows2(w_outer[j * per : (j + 1) * per]), NT)
            d_inner = (d_act * gp[i, :, cols].astype(F32)).astype(BF16)
            gp[i, :, cols] = d_inner
            add_row(8 + j, d_inner.astype(F32))
            term = mm(d_inner, rows2(w_inner[:, :, :, cols]), NT)
            back = term if back is None else back + term
        for one in row_copies(i, 1):
            one.start()
        d_first_out = ds[...] + back
        normed = nf[i]
        add_row(3, d_first_out * normed)
        add_row(4, d_first_out)
        d_first = norm_back(d_first_out, normed, inv[i], g_first)
        dfi[slot] = d_first
        low = d_first.astype(BF16)
        dbr[slot] = low
        add_row(2, low.astype(F32))
        for one in row_copies(i, 2):
            one.start()

    if remote:
        for unit in units:
            unit.drain()
        for short in shorts:
            short.wait_send()
        for one in whole_copies:
            one.wait()
    for i in range(n_tiles):
        for which in (0, 1, 2) if i >= n_tiles - 2 else (0, 1):
            for one in row_copies(i, which):
                one.wait()
    for h in range(max(0, heads - 2), heads):
        head_copy(h, h % 2).wait()
    xt_copy.wait()
    att_copy.wait()


def fwd_call(remote, x, w_in, w_out, w_inner, w_outer, vec, seg, ok, qperm, kperm, cot):
    length, width = x.shape
    heads = qperm.shape[0]
    hd = width // heads
    ff = w_inner.shape[-1]
    groups = heads // HG
    wholes = [(groups, 8, 2, width // 16, 3 * HG * hd)] + [(8, 2, w.shape[-2], w.shape[-1]) for w in (w_out, w_inner, w_outer)]
    tm = 256
    n_tiles = length // tm
    hbm = pl.BlockSpec(memory_space=pl.ANY)
    vmem = pl.BlockSpec(memory_space=pltpu.VMEM)
    outs = [
        ((length, width), BF16), ((length, ff), BF16), ((length, ff), BF16), ((length, width), BF16), ((length, width), BF16),
        ((length, width), F32), ((length, width), BF16), ((width, length), BF16), ((heads, 3 * hd + CL, length), BF16),
        ((width, length), BF16), ((16, width), F32),
    ]
    if remote:
        outs += [(wholes[0], BF16), (wholes[1], BF16)]
    scratch = [
        ((length, width), BF16), ((length, width), BF16), *[(whole, BF16) for whole in wholes],
        ((3 * HG * hd, length), BF16), ((width, 16), F32), ((16, length), BF16), ((16, length), BF16), ((length, length), BF16), ((length, length), BF16),
        ((width, length), BF16), ((2, 3 * hd + CL, length), BF16), ((width, length), BF16),
        ((n_tiles, tm, ff), BF16), ((n_tiles, tm, ff), BF16), ((n_tiles, tm, width), BF16), ((n_tiles, tm, width), F32), ((n_tiles, tm, width), F32),
        ((n_tiles, tm, 1), F32), ((2, tm, width), BF16), ((2, tm, width), F32), ((2, tm, width), BF16), ((2, tm, width), BF16), ((tm, width), F32),
    ]
    sems = [(5 + 3 * groups,), (n_tiles, 3), (2, 4), (2,), (2,)]
    extra = []
    if remote:
        n_shard, units = lax.axis_size("shard"), len(GATHERED)
        extra = [pltpu.VMEM((n_shard, 16, width), BF16)]
        extra += [pltpu.SemaphoreType.DMA(n) for n in ((units, GATHER_SEMS), (units, GATHER_SEMS), (n_shard,), (n_shard,), (2,))]
    return pl.pallas_call(
        partial(fwd_kernel, heads, remote),
        out_shape=[jax.ShapeDtypeStruct(s, d) for s, d in outs],
        in_specs=[hbm] * 5 + [vmem] * 5 + [hbm],
        out_specs=[hbm] * 10 + [vmem] + [hbm] * (len(outs) - 11),
        scratch_shapes=[pltpu.VMEM(s, d) for s, d in scratch] + [pltpu.SemaphoreType.DMA(n) for n in sems] + extra,
        compiler_params=pltpu.CompilerParams(vmem_limit_bytes=63_400_000, collective_id=0 if remote else None, has_side_effects=remote),
        name="layer_forward",
    )(x, w_in, w_out, w_inner, w_outer, vec, seg, ok, qperm, kperm, cot)


SUMMED = [("outer", n * 48, 0, 384, "xy"[n % 2]) for n in range(4)]
SUMMED += [("inner", 0, n * 384, 384, "xy"[n % 2]) for n in range(4)]
SUMMED += [("out", 0, 0, 384, "x"), ("in0", 0, 0, 384, "y"), ("in1", 0, 0, 384, "x"), ("in2", 0, 0, 256, "x"), ("in2", 0, 256, 128, "y")]
SUM_STAGES = ("core", "first", "second", "third", "fourth", "fifth", "last")
AT_INNER = {0: [(0, 0), (0, 1), (0, 2), (0, 3)], 5: [(1, 0), (1, 1)]}
AT_ATTENDED = [(0, 4), (0, 5), (0, 6), (0, 7)]
AT_BACK_HEAD = {
    0: [(0, 8), (1, 2), (1, 3)],
    1: [(2, 0), (2, 1)],
    2: [(1, 4), (1, 5)],
    3: [(3, 0), (3, 1), (2, 2), (2, 3)],
    4: [(0, 9), (1, 6), (1, 7)],
    5: [(3, 2), (3, 3), (2, 4), (2, 5)],
    6: [(4, 0), (4, 1), (1, 8)],
    7: [(3, 4), (3, 5)],
    8: [(0, 10), (2, 6), (2, 7), (1, 9), (5, 0), (5, 1), (4, 2), (4, 3)],
    9: [(2, 8), (4, 4), (4, 5)],
    10: [(3, 6), (3, 7), (1, 10), (5, 2), (5, 3)],
    11: [(2, 9), (3, 8), (5, 4), (5, 5)],
}
AT_GRAD = {
    0: [(0, 11), (0, 12), (2, 10), (4, 6), (4, 7)],
    1: [(1, 11), (1, 12), (3, 9), (4, 8)],
    2: [(3, 10), (5, 6), (5, 7), (5, 8)],
    3: [(2, 11), (2, 12), (4, 9)],
}
AT_END = [
    (4, 10), (3, 11), (3, 12), (5, 9), (5, 10), (4, 11), (4, 12), (5, 11), (5, 12),
]


def bwd_kernel(heads, remote, *refs):
    (act_hbm, din_hbm, flow_hbm, dou_hbm, dfi_hbm, dbr_hbm, att_hbm, head_hbm, xt_hbm, w_in_hbm, w_out_hbm, qperm_ref, kperm_ref, vg_ref), refs = (
        refs[:14], refs[14:]
    )
    (ig_hbm, vgrad_ref, *grad_outs), refs = refs[:6], refs[6:]
    (act, din, flow, dou, dfi, att, head, xt, w_in, w_out, ptq, ptk, mixed, dproj), refs = refs[:14], refs[14:]
    (g_outer, g_inner, g_out, g_in), refs = refs[:4], refs[4:]
    (ig, in_sem, act_sem, din_sem, head_sem, dfi_sem, ig_sem, out_sem), refs = refs[:8], refs[8:]
    dbr = flow
    length, width = flow.shape
    hd = width // heads
    groups = heads // HG
    gw = HG * hd
    tm = ig.shape[1]
    fc = act.shape[2]
    ic = din.shape[2]
    copy = pltpu.make_async_copy
    n_act = act_hbm.shape[1] // fc
    n_din = din_hbm.shape[1] // ic
    n_tiles = length // tm
    acts = [copy(act_hbm.at[:, j * fc : (j + 1) * fc], act.at[j % 2], act_sem.at[j % 2]) for j in range(n_act)]
    dins = [copy(din_hbm.at[:, j * ic : (j + 1) * ic], din.at[j % 2], din_sem.at[j % 2]) for j in range(n_din)]
    dfis = [copy(dfi_hbm.at[i * tm : (i + 1) * tm, :], dfi.at[i % 2], dfi_sem.at[i % 2]) for i in range(n_tiles)]
    loads = {
        name: copy(s, d, in_sem.at[i])
        for i, (name, s, d) in enumerate(
            (
                ("dou", dou_hbm, dou), ("flow", flow_hbm, flow), ("dbr", dbr_hbm, dbr), ("w_out", w_out_hbm, w_out),
                ("att", att_hbm, att), ("xt", xt_hbm, xt.at[:width, :]), ("w_in", w_in_hbm, w_in),
            )
        )
    }

    def head_copy(h, slot):
        return copy(head_hbm.at[h], head.at[slot], head_sem.at[slot])

    loads["dou"].start()
    acts[0].start()
    acts[1].start()
    loads["flow"].start()
    dins[0].start()
    dins[1].start()
    for name in ("w_out", "att", "xt", "w_in"):
        loads[name].start()
    head_copy(0, 0).start()
    dfis[0].start()
    dfis[1].start()

    if remote:
        sum_outs, (vslots, vsum, vsend, vrecv, send, recv, *buffers) = refs[:4], refs[4:]
        p = Place()
        barrier = pltpu.get_barrier_semaphore()
        for other in (p.sibling, p.across):
            pl.semaphore_signal(barrier, inc=1, device_id={"rep": other}, device_id_type=pl.DeviceIdType.MESH)
        for other in [p.beside] + [p.plane(dz) * 2 + p.y for dz in (1, 2, 3)]:
            pl.semaphore_signal(barrier, inc=1, device_id={"shard": other}, device_id_type=pl.DeviceIdType.MESH)
        parts = {"outer": (g_outer, sum_outs[0]), "inner": (g_inner, sum_outs[1]), "out": (g_out, sum_outs[2])}
        parts.update({"in%d" % g: (g_in.at[g], sum_outs[3].at[g]) for g in range(groups)})
        units = [
            Scatter(p, *parts[name], slice(row, row + 48), start, size, kind, buffers[4 * u : 4 * u + 4], send.at[u], recv.at[u])
            for u, (name, row, start, size, kind) in enumerate(SUMMED)
        ]

        def pump(steps):
            for stage, u in steps:
                getattr(units[u], SUM_STAGES[stage])()
    else:
        def pump(steps):
            pass

    loads["dou"].wait()
    for j in range(n_act):
        acts[j].wait()
        part = mm(act[j % 2], dou[...], TN)
        g_outer[j] = part.astype(BF16).reshape(g_outer.shape[1:])
        if j + 2 < n_act:
            acts[j + 2].start()
    if remote:
        pl.semaphore_wait(barrier, 6)

    loads["flow"].wait()
    mixed[...] = flow[...].T
    loads["dbr"].start()
    for j in range(n_din):
        pump(AT_INNER.get(j, ()))
        dins[j].wait()
        part = mm(mixed[...], din[j % 2], NN)
        g_inner[:, :, :, j * ic : (j + 1) * ic] = part.astype(BF16).reshape(g_inner.shape[:3] + (ic,))
        if j + 2 < n_din:
            dins[j + 2].start()
    pump(AT_ATTENDED)

    for name in ("dbr", "w_out", "att"):
        loads[name].wait()
    mixed[...] = mm(rows2(w_out[...]), dbr[...], NT).astype(BF16)
    g_out[...] = mm(att[...], dbr[...], NN).astype(BF16).reshape(g_out.shape)

    cols = [slice(c * CL, (c + 1) * CL) for c in range(length // CL)]

    def attend(h):
        slot = lax.rem(h, 2)
        one_hot(qperm_ref, h, ptq)
        one_hot(kperm_ref, h, ptk)
        d_arr = mm(mixed[pl.ds(pl.multiple_of(h * hd, hd), hd), :], ptq[...], NN).astype(BF16)
        head_copy(h, slot).wait()

        @pl.when(h + 1 < heads)
        def _():
            head_copy(h + 1, 1 - slot).start()

        q_arr = head[slot, :hd, :]
        k_arr = head[slot, hd : 2 * hd, :]
        v_arr = head[slot, 2 * hd : 3 * hd, :]
        probs = head[slot, 3 * hd :, :]
        d_probs = jnp.concatenate([mm(v_arr[:, c], d_arr[:, c], TN) for c in cols], axis=1)
        wide = probs.astype(F32)
        terms = jnp.sum(wide * d_probs, axis=0, keepdims=True)
        d_scores = (wide * (d_probs - terms)).astype(BF16)
        dq = jnp.concatenate([mm(k_arr[:, c], d_scores[:, c], NN) for c in cols], axis=1) * 0.125
        dk = jnp.concatenate([mm(q_arr[:, c], d_scores[:, c], NT) for c in cols], axis=1)
        dv = jnp.concatenate([mm(d_arr[:, c], probs[:, c], NT) for c in cols], axis=1)
        base = (h // HG) * 3 * gw + lax.rem(h, HG) * hd
        dproj[pl.ds(pl.multiple_of(base, hd), hd), :] = mm(dq.astype(BF16), ptq[...], NT).astype(BF16)
        dkv = mm(jnp.concatenate([dk, dv], axis=0).astype(BF16), ptk[...], NT).astype(BF16)
        dproj[pl.ds(pl.multiple_of(base + gw, hd), hd), :] = dkv[:hd, :]
        dproj[pl.ds(pl.multiple_of(base + 2 * gw, hd), hd), :] = dkv[hd:, :]

    loads["xt"].wait()
    xt[width:, :] = jnp.where(lax.broadcasted_iota(jnp.int32, (16, length), 0) == 0, 1.0, 0.0).astype(BF16)
    vgrad_ref[...] = vg_ref[...]

    @pl.loop(0, heads)
    def _(h):
        for at in AT_BACK_HEAD if remote else ():
            @pl.when(h == at)
            def _():
                pump(AT_BACK_HEAD[at])

        attend(h)

        @pl.when(lax.rem(h, HG) == HG - 1)
        def _():
            g = h // HG
            prod = mm(xt[...], dproj[pl.ds(pl.multiple_of(g * 3 * gw, gw), 3 * gw), :], NT)
            g_in[g] = prod[:width].astype(BF16).reshape(g_in.shape[1:])
            where = pl.ds(pl.multiple_of(g * gw, gw), gw)
            vgrad_ref[0:1, where] = prod[width : width + 1, :gw]
            vgrad_ref[1:2, where] = prod[width : width + 1, 2 * gw :]

    def vector_stage(n, axis, others):
        copies = [rcopy(vsum, vslots.at[n + i], vsend.at[n + i], vrecv.at[n + i], axis, other) for i, other in enumerate(others)]
        for one in copies:
            one.start()

        def wait():
            for one in copies:
                one.wait()
            total = vsum[...]
            for i in range(len(others)):
                total = total + vslots[n + i]
            vsum[...] = total

        return wait

    if not remote:
        outs = [copy(s, d, out_sem.at[i]) for i, (s, d) in enumerate(zip((g_outer, g_inner, g_out, g_in), grad_outs))]
        for out in outs:
            out.start()
    loads["w_in"].wait()
    stores = [copy(ig.at[i % 2], ig_hbm.at[i * tm : (i + 1) * tm, :], ig_sem.at[i % 2]) for i in range(n_tiles)]
    if remote:
        planes = [p.plane(dz) * 2 + p.y for dz in (3, 2, 1)]
        vector_steps = [(0, "rep", [p.sibling]), (1, "rep", [p.across]), (2, "shard", [p.beside]), (3, "shard", planes)]
        vsum[...] = vgrad_ref[...]
    for i in range(n_tiles):
        if remote:
            if i:
                vector_wait()
            pump(AT_GRAD.get(i, ()))
            if i < len(vector_steps):
                vector_wait = vector_stage(*vector_steps[i])
        prod = mm(rows2(w_in[0]), dproj[: 3 * gw, i * tm : (i + 1) * tm], NN)
        for g in range(1, groups):
            prod = prod + mm(rows2(w_in[g]), dproj[g * 3 * gw : (g + 1) * 3 * gw, i * tm : (i + 1) * tm], NN)
        dfis[i].wait()
        if i >= 2:
            stores[i - 2].wait()
        ig[i % 2] = (dfi[i % 2] + prod.T).astype(BF16)
        stores[i].start()
        if i + 2 < n_tiles:
            dfis[i + 2].start()
    if remote:
        for i in range(n_tiles, len(vector_steps)):
            vector_wait()
            vector_wait = vector_stage(*vector_steps[i])
        pump(AT_END)
        vector_wait()
        vgrad_ref[...] = vsum[...]
        for unit in units:
            unit.last()
        outs = [copy(s, d, out_sem.at[i]) for i, (s, d) in enumerate(zip(sum_outs[:3], grad_outs))]
        outs += [
            copy(
                sum_outs[3].at[g, :, :, pl.ds(q * gw, gw)], grad_outs[3].at[:, :, pl.ds(q * width + g * gw, gw)], out_sem.at[3 + 3 * g + q]
            )
            for g in range(groups)
            for q in range(3)
        ]
        for out in outs:
            out.start()
        for unit in units:
            unit.drain()
    for i in range(max(0, n_tiles - 2), n_tiles):
        stores[i].wait()
    for out in outs:
        out.wait()


def bwd_call(remote, act, din, flow, dou, dfi, dbr, att, head, xt, w_in, w_out, qperm, kperm, vgrad):
    length, width = flow.shape
    heads = qperm.shape[0]
    hd = width // heads
    ff = act.shape[1]
    groups = heads // HG
    tm = 256
    hbm = pl.BlockSpec(memory_space=pl.ANY)
    vmem = pl.BlockSpec(memory_space=pltpu.VMEM)
    gshapes = [(8, 2, ff // 16, width), (8, 2, width // 16, ff), (8, 2, width // 16, width), (groups, 8, 2, width // 16, 3 * HG * hd)]
    fc = ff // 8
    if remote:
        finals = [shape[1:] for shape in gshapes[:3]] + [(2, width // 16, 3 * width)]
    else:
        finals = gshapes
    outs = [((length, width), BF16), ((16, width), F32)] + [(shape, BF16) for shape in finals]
    scratch = [
        ((2, length, fc), BF16), ((2, length, fc), BF16), ((length, width), BF16), ((length, width), BF16), ((2, tm, width), F32),
        ((width, length), BF16), ((2,) + head.shape[1:], BF16), ((width + 16, length), BF16), (w_in.shape, BF16), (w_out.shape, BF16),
        ((length, length), BF16), ((length, length), BF16), ((width, length), BF16), ((3 * width, length), BF16),
    ] + [(s, BF16) for s in gshapes] + [((2, tm, width), BF16)]
    sems = [(7,), (2,), (2,), (2,), (2,), (2,), (3 + 3 * groups,)]
    extra = []
    if remote:
        extra += [pltpu.VMEM(s, BF16) for s in [s[1:] for s in gshapes[:3]] + [(groups,) + gshapes[3][2:]]]
        extra += [pltpu.VMEM((6, 16, width), F32), pltpu.VMEM((16, width), F32)]
        extra += [pltpu.SemaphoreType.DMA(n) for n in ((6,), (6,), (len(SUMMED), SCATTER_SEMS), (len(SUMMED), SCATTER_SEMS))]
        for _, _, _, size, _ in SUMMED:
            extra += [pltpu.VMEM(s, BF16) for s in scatter_buffers(width // 16, size)]
    return pl.pallas_call(
        partial(bwd_kernel, heads, remote),
        out_shape=[jax.ShapeDtypeStruct(s, d) for s, d in outs],
        in_specs=[hbm] * 11 + [vmem] * 3,
        out_specs=[hbm, vmem] + [hbm] * 4,
        scratch_shapes=[pltpu.VMEM(s, d) for s, d in scratch] + [pltpu.SemaphoreType.DMA(n) for n in sems] + extra,
        compiler_params=pltpu.CompilerParams(vmem_limit_bytes=63_400_000, collective_id=1 if remote else None, has_side_effects=remote),
        name="layer_backward",
    )(act, din, flow, dou, dfi, dbr, att, head, xt, w_in, w_out, qperm, kperm, vgrad)


def shards(
    layer_input, in_weight, query_bias, value_bias, out_weight, out_bias, first_gain, first_shift, inner_weight, inner_bias,
    outer_weight, outer_bias, second_gain, second_shift, segment_ids, token_valid, query_perm, key_perm, out_cotangent,
):
    _, length, width = layer_input.shape
    heads = query_perm.shape[1]
    ff = inner_weight.shape[1]
    n_shard = lax.axis_size("shard")
    shard = lax.axis_index("shard")

    piece = width // n_shard
    groups = heads // HG
    remote = n_shard == 8 and lax.axis_size("rep") == 4

    def whole(rows):
        return lax.all_gather(rows, "shard", axis=0, tiled=True)

    def blocked(rows):
        return rows.reshape(8, 2, rows.shape[0] // 16, rows.shape[1])

    def halved(rows):
        return rows.reshape(2, rows.shape[0] // 2, rows.shape[1])

    weights = (in_weight, out_weight, inner_weight, outer_weight)
    short = jnp.stack([query_bias, value_bias, out_bias, first_gain, first_shift, outer_bias, second_gain, second_shift])
    inner_piece = ff // n_shard
    if remote:
        w_in, w_out, w_inner, w_outer = [halved(w) for w in weights]
        vec = lax.dynamic_update_slice(jnp.zeros((16, width), BF16), short, (0, shard * piece))
        first = shard * inner_piece
        vec = lax.dynamic_update_slice(vec, inner_bias[None], (8 + first // width, first % width))
    else:
        w_in, w_out, w_inner, w_outer = [whole(w) for w in weights]
        w_in = jnp.transpose(w_in.reshape(width, 3, groups, -1), (2, 0, 1, 3)).reshape(groups, 8, 2, width // 16, -1)
        w_out, w_inner, w_outer = [blocked(w) for w in (w_out, w_inner, w_outer)]
        vectors = lax.all_gather(jnp.concatenate([short.reshape(-1), inner_bias]), "shard", axis=0)
        vec = jnp.concatenate(
            [
                jnp.transpose(vectors[:, : 8 * piece].reshape(n_shard, 8, piece), (1, 0, 2)).reshape(8, width),
                vectors[:, 8 * piece :].reshape(ff // width, width),
                jnp.zeros((8 - ff // width, width), BF16),
            ]
        )
    hidden, act, din, flow, dou, dfi, dbr, att, head, xt, vg, *wholes = fwd_call(
        remote, layer_input[0], w_in, w_out, w_inner, w_outer, vec, segment_ids, token_valid, query_perm[0], key_perm[0], out_cotangent[0]
    )
    if remote:
        w_in, w_out = wholes
    grad_x, vg, g_outer, g_inner, g_out, g_in = bwd_call(
        remote, act, din, flow, dou, dfi, dbr, att, head, xt, w_in, w_out, query_perm[0], key_perm[0], vg
    )
    if not remote:
        g_in = jnp.transpose(g_in.reshape(groups, width, 3, -1), (1, 2, 0, 3))
    grads = [g_in.reshape(-1, 3 * width), g_out.reshape(-1, width), g_inner.reshape(-1, ff), g_outer.reshape(-1, width)]

    def summed(grad):
        rows = lax.psum_scatter(grad.astype(F32), "shard", scatter_dimension=0, tiled=True)
        return lax.psum(rows.astype(BF16), "rep").astype(F32)

    if remote:
        d_in, d_out, d_inner, d_outer = [g.astype(F32) for g in grads]
    else:
        d_in, d_out, d_inner, d_outer = [summed(g) for g in grads]
        vg = lax.psum(vg, ("rep", "shard"))
    mine = lax.dynamic_slice(vg, (0, shard * piece), (8, piece))
    inner_mine = lax.dynamic_slice(vg[8 : 8 + ff // width].reshape(ff), (shard * inner_piece,), (inner_piece,))
    return (
        hidden[None], grad_x[None], d_in, mine[0], mine[1], d_out, mine[2], mine[3], mine[4], d_inner, inner_mine, d_outer,
        mine[5], mine[6], mine[7],
    )


def solution(mesh):
    rows, vector = P("shard", None), P("shard")
    seq2, seq3 = P(("rep", "shard"), None), P(("rep", "shard"), None, None)
    return jax.shard_map(
        shards,
        mesh=mesh,
        in_specs=(
            seq3, rows, vector, vector, rows, vector, vector, vector, rows, vector, rows, vector, vector, vector, seq2, seq2, seq3, seq3, seq3,
        ),
        out_specs=(seq3, seq3, rows, vector, vector, rows, vector, vector, vector, rows, vector, rows, vector, vector, vector),
        check_vma=False,
    )
```

time: 1030 us -> 253 us (0.25)
  waiting for transfers between devices: 732 us -> 0 us
  Pallas kernels: 142 us -> 233 us
  blocking collectives: 72.7 us -> 0 us
  local copies, waits for them, and re-layouts: 35.1 us -> 9.48 us
  other arithmetic: 29.3 us -> 5.97 us
  between operations: 14.1 us -> 1.19 us
    reduce_scatter x3 -> x0, waiting for transfers between devices: 355 us -> none  [summed(): lax.psum_scatter(grad.astype(F32), 'shard', scatter_dimension=0, tiled=True)]
    all_gather x4 -> x0, waiting for transfers between devices: 234 us -> none  [whole(): return lax.all_gather(rows, 'shard', axis=0, tiled=True)]
    unnamed x10 -> x0, waiting for transfers between devices: 133 us -> none
    pallas_call x2, Pallas kernels: 142 us -> 233 us  [the longest x1 124 us: fwd_call(): pl.pallas_call(partial(fwd_kernel, heads, remote), out_shape=[jax.ShapeDt...]
    psum x1 -> x0, blocking collectives: 40.3 us -> none  [shards(): vg = lax.psum(vg, ('rep', 'shard'))]
    all_gather x1 -> x0, blocking collectives: 32.4 us -> none  [shards(): lax.all_gather(jnp.concatenate([short.reshape(-1), inner_bias]), 'shard',...]
    convert_element_type x9 -> x4, other arithmetic: 27.9 us -> 5.97 us  [shards(): d_in, d_out, d_inner, d_outer = [g.astype(F32) for g in grads]]
    convert_element_type x2 -> x0, local copies, waits for them, and re-layouts: 18.6 us -> none  [summed(): grad.astype(F32)]
  transfers between devices with their start and end apart: 9 -> 0, of which waited for: 9 -> 0; matrix products, arithmetic and copies ran while one was open for 5% -> 0% of each run, Pallas kernels for 0% -> 0%
where the time goes in v3:
time: 253 us; the launch traced here: 250 us
  Pallas kernels  233 us (92%)
  local copies, waits for them, and re-layouts  9.48 us (4%)
  other arithmetic  5.97 us (2%)
    pallas_call x1, Pallas kernels, fwd_call(): pl.pallas_call(partial(fwd_kernel, heads, remote), out_shape=[jax.ShapeDt...  124 us
    pallas_call x1, Pallas kernels, bwd_call(): pl.pallas_call(partial(bwd_kernel, heads, remote), out_shape=[jax.ShapeDt...  109 us
    convert_element_type x4, other arithmetic, shards(): d_in, d_out, d_inner, d_outer = [g.astype(F32) for g in grads]  5.97 us

profile of v3, /device:TPU:0, one launch (start us, length us, event | category | flops | bytes accessed | tf_op | source)
XLA Modules:
  0.0 249.6 jit_solution(16196100809689178417)
XLA Ops:
  0.7 0.7 broadcast_in_dim.13
  1.4 0.8 stack.35
  2.2 0.3 dynamic_update_slice.6
  2.5 0.3 dynamic_update_slice.7.refs_5_
  2.8 0.0 copy-start.4
  2.8 1.5 copy_bitcast_fusion
  4.3 0.0 copy-done.4
  4.3 124.1 %layer_forward.1 = (bf16[1024,768]{1,0:T(8,128)(2,1)}, bf16[1024,3072]{1,0:T(8,128)(2,1)}, bf16[1024,3072]{1,0:T(8,128)(2,1)}, bf16[1024,768]{1,0:T(8,128)(2,1)}...) custom-call(bf16[1024,768]{1,0:T(8,128)(2,1)} %bitcast.48, ...), custom_call_target="tpu_custom_call" | custom-call | tf_op jit(solution)/shard_map/layer_forward/pallas_call | solution.py:552
  128.4 108.8 %layer_backward.1 = (bf16[1024,768]{1,0:T(8,128)(2,1)}, f32[16,768]{1,0:T(8,128)}, bf16[2,192,768]{2,1,0:T(8,128)(2,1)}, bf16[2,48,3072]{2,1,0:T(8,128)(2,1)}, b...) custom-call(bf16[1024,3072]{1,0:T(8,128)(2,1)} %get-tuple-element.35.refs_0_, ...), custom_call_target="tpu_custom_call" | custom-call | tf_op jit(solution)/shard_map/layer_backward/pallas_call | solution.py:841
  237.3 0.0 copy-start.3
  237.3 0.8 constant_dynamic-slice_fusion
  238.1 0.7 slice.32
  238.9 0.7 dynamic_slice.7
  239.5 0.5 slice_bitcast_fusion
  240.1 1.6 bitcast_convert_fusion.3
  241.7 0.0 copy-start.2
  241.7 2.0 bitcast_convert_fusion.2
  243.8 0.0 copy-done.3
  243.8 0.0 copy-start
  243.8 1.2 bitcast_convert_fusion.1
  244.9 0.0 copy-done.2
  244.9 1.1 bitcast_convert_fusion
  246.0 0.0 copy-done
  246.0 0.0 copy-start.1
  246.0 1.1 copy.42
  247.2 0.8 copy-done.1
  248.0 1.1 copy.43
  (2 shorter events, 0.0 us)
Async XLA Ops:
  2.8 1.5 copy-start.4
  237.3 6.5 %copy-start.3 = (bf16[2,48,3072]{2,1,0:T(8,128)(2,1)S(1)}, bf16[2,48,3072]{2,1,0:T(8,128)(2,1)}, u32[]{:S(2)}) copy-start(bf16[2,48,3072]{2,1,0:T(8,128)(2,1)} %get-tuple-element.51) | copy-start | bytes 1769476
  241.7 3.2 %copy-start.2 = (bf16[2,192,768]{2,1,0:T(8,128)(2,1)S(1)}, bf16[2,192,768]{2,1,0:T(8,128)(2,1)}, u32[]{:S(2)}) copy-start(bf16[2,192,768]{2,1,0:T(8,128)(2,1)} %get-tuple-element.52) | copy-start | bytes 1769476
  243.8 2.3 copy-start
  246.0 2.0 copy-start.1

commit v4 on v3

--- a/solution.py
+++ b/solution.py
@@ -232,7 +232,7 @@
 
 def one_hot(perm_ref, h, pt_ref):
     length = pt_ref.shape[0]
-    row = perm_ref[pl.ds(h, 1), :].astype(jnp.int16)
+    row = perm_ref[h].astype(jnp.int16)
     places = lax.broadcasted_iota(jnp.int16, (length, length), 0)
     pt_ref[...] = jnp.where(places == row, jnp.ones((), BF16), jnp.zeros((), BF16))
 
@@ -243,13 +243,42 @@
 GATHERED += [("inner", 0, n * 384, 384, "yx"[n % 2]) for n in range(4)]
 GATHERED += [("outer", n * 48, 0, 384, "xxyx"[n]) for n in range(4)]
 IN0, IN1, IN2, OUT, INNER, OUTER = [0, 1], [2], [3], [4], [5, 6, 7, 8], [9, 10, 11, 12]
-AT_START = [(1, 0), (1, 1)]
-AHEAD = [(2, 0), (1, 2), (2, 1), (1, 3), (3, 0), (3, 1), (2, 2), (1, 4), (4, 0), (4, 1), (2, 3), (1, 5), (5, 0), (5, 1)]
-AT_HEAD = {1: [(3, 2), (3, 3), (2, 4), (2, 5), (1, 6), (1, 7)], 3: [(4, 2), (2, 6), (1, 8)], 4: [(4, 3), (5, 2)], 5: [(3, 4), (3, 5), (2, 7), (2, 8), (1, 9), (1, 10)], 6: [(3, 6)], 7: [(4, 4), (2, 9), (1, 11)], 8: [(4, 5), (3, 7), (2, 10), (1, 12), (5, 3)], 9: [(4, 6), (3, 8), (2, 11)], 10: [(3, 9), (2, 12)]}
-AT_FFN = [(5, 4), (5, 5), (5, 6), (4, 7), (5, 7), (4, 8), (5, 8)]
-AT_TILE = {0: [(3, 10), (3, 11), (4, 9)], 1: [(4, 10), (3, 12)], 2: [(4, 11), (4, 12)]}
+AT_START = [(1, 0), (1, 1), (1, 2)]
+AHEAD_A = [(2, 0), (1, 3), (2, 1), (1, 4), (2, 2), (1, 5), (3, 0), (3, 1), (2, 3), (1, 6), (3, 2), (2, 4), (1, 7)]
+AHEAD_B = [(4, 0), (4, 1), (5, 0), (5, 1)]
+AT_HEAD = {0: [(3, 3), (2, 5), (1, 8)], 1: [(4, 2), (2, 6), (3, 4), (2, 7), (1, 9), (1, 10)], 2: [(3, 5)], 3: [(4, 3), (2, 8), (1, 11)], 4: [(4, 4), (3, 6), (2, 9), (1, 12), (5, 2)], 5: [(3, 7), (2, 10), (2, 11)], 6: [(4, 5)], 7: [(4, 6), (3, 8), (2, 12)], 8: [(3, 9), (5, 3)], 11: [(4, 7), (4, 8)]}
+AT_FFN = [(3, 10), (3, 11), (5, 4), (5, 5), (5, 6), (5, 7), (5, 8)]
+AT_TILE = {1: [(4, 9), (3, 12)], 2: [(4, 10), (4, 11)], 3: [(4, 12)]}
 AT_BACK = [(5, 9), (5, 10), (5, 11), (5, 12)]
 STAGES = ("", "first", "second", "third", "fourth", "last")
+
+
+def placed(p, vslots, shorts, width, ff):
+    n_shard = len(shorts) + 1
+    piece = width // n_shard
+    lanes = vslots.shape[2]
+    per_row = width // piece
+    for short in shorts:
+        short.wait_recv()
+    slots = [vslots[m] for m in range(n_shard)]
+    joined = jnp.concatenate(slots, axis=1)
+    shape = (n_shard * lanes, width)
+    source = lax.broadcasted_iota(jnp.int32, shape, 0)
+    offset = lax.broadcasted_iota(jnp.int32, shape, 1) - source % lanes
+    owner = (source // lanes + p.shard) % n_shard
+    offset = jnp.where(source % lanes < piece, offset, -1)
+    spread = jnp.where(offset == owner * piece, 1.0, 0.0).astype(BF16)
+    vec = mm(joined, spread, NN)
+    rows = lax.broadcasted_iota(jnp.int32, (16, joined.shape[1]), 0)
+    owners = (lax.broadcasted_iota(jnp.int32, (16, joined.shape[1]), 1) // lanes + p.shard) % n_shard
+    repeats = ff // width
+    result = jnp.where(lax.broadcasted_iota(jnp.int32, vec.shape, 0) < 8, vec, 0.0)
+    for r in range(repeats):
+        chunk = owners * repeats + r
+        left = jnp.where(rows == 8 + chunk // per_row, joined[8 + r : 9 + r, :].astype(F32), 0.0).astype(BF16)
+        spread = jnp.where(offset == (owner * repeats + r) % per_row * piece, 1.0, 0.0).astype(BF16)
+        result = result + mm(left, spread, NN)
+    return result
 
 
 def fwd_kernel(heads, remote, *refs):
@@ -272,6 +301,8 @@
     pairs = ((w_out_hbm, w_out), (w_inner_hbm, w_inner), (w_outer_hbm, w_outer))
     if remote:
         vslots, send, recv, vsend, vrecv, whole_sem = refs
+        vslots[0] = jnp.zeros(vslots.shape[1:], BF16)
+        vslots[0, : vec_ref.shape[0], : vec_ref.shape[1]] = vec_ref[...]
         p = Place()
         n_shard = lax.axis_size("shard")
         owns = [
@@ -295,7 +326,7 @@
             for u, (name, row, start, size, kind) in enumerate(GATHERED)
         ]
         shorts = [
-            rcopy(vec_ref, vslots.at[n_shard - d], vsend.at[n_shard - d], vrecv.at[n_shard - d], "shard", (p.shard + d) % n_shard)
+            rcopy(vslots.at[0], vslots.at[n_shard - d], vsend.at[n_shard - d], vrecv.at[n_shard - d], "shard", (p.shard + d) % n_shard)
             for d in range(1, n_shard)
         ]
 
@@ -329,14 +360,12 @@
     xt[...] = xv[...].T
     xt_copy = copy(xt, xt_hbm, once_sem.at[0])
     xt_copy.start()
-    vec = vec_ref[...].astype(F32)
-    if remote:
-        for short in shorts:
-            short.wait_recv()
-        for d in range(1, n_shard):
-            vec = vec + vslots[d].astype(F32)
-        pump(AHEAD)
+    if remote:
+        pump(AHEAD_A)
+        vec = placed(p, vslots, shorts, width, ff)
+        pump(AHEAD_B)
     else:
+        vec = vec_ref[...].astype(F32)
         for own in owns:
             own.wait()
     vcol[...] = vec.T
@@ -547,7 +576,7 @@
     extra = []
     if remote:
         n_shard, units = lax.axis_size("shard"), len(GATHERED)
-        extra = [pltpu.VMEM((n_shard, 16, width), BF16)]
+        extra = [pltpu.VMEM((n_shard, 16, 128), BF16)]
         extra += [pltpu.SemaphoreType.DMA(n) for n in ((units, GATHER_SEMS), (units, GATHER_SEMS), (n_shard,), (n_shard,), (2,))]
     return pl.pallas_call(
         partial(fwd_kernel, heads, remote),
@@ -564,31 +593,12 @@
 SUMMED += [("inner", 0, n * 384, 384, "xy"[n % 2]) for n in range(4)]
 SUMMED += [("out", 0, 0, 384, "x"), ("in0", 0, 0, 384, "y"), ("in1", 0, 0, 384, "x"), ("in2", 0, 0, 256, "x"), ("in2", 0, 256, 128, "y")]
 SUM_STAGES = ("core", "first", "second", "third", "fourth", "fifth", "last")
-AT_INNER = {0: [(0, 0), (0, 1), (0, 2), (0, 3)], 5: [(1, 0), (1, 1)]}
+AT_INNER = {0: [(0, 0), (0, 1), (0, 2), (0, 3)], 4: [(1, 0), (1, 1)], 5: [(1, 2), (1, 3)]}
 AT_ATTENDED = [(0, 4), (0, 5), (0, 6), (0, 7)]
-AT_BACK_HEAD = {
-    0: [(0, 8), (1, 2), (1, 3)],
-    1: [(2, 0), (2, 1)],
-    2: [(1, 4), (1, 5)],
-    3: [(3, 0), (3, 1), (2, 2), (2, 3)],
-    4: [(0, 9), (1, 6), (1, 7)],
-    5: [(3, 2), (3, 3), (2, 4), (2, 5)],
-    6: [(4, 0), (4, 1), (1, 8)],
-    7: [(3, 4), (3, 5)],
-    8: [(0, 10), (2, 6), (2, 7), (1, 9), (5, 0), (5, 1), (4, 2), (4, 3)],
-    9: [(2, 8), (4, 4), (4, 5)],
-    10: [(3, 6), (3, 7), (1, 10), (5, 2), (5, 3)],
-    11: [(2, 9), (3, 8), (5, 4), (5, 5)],
-}
-AT_GRAD = {
-    0: [(0, 11), (0, 12), (2, 10), (4, 6), (4, 7)],
-    1: [(1, 11), (1, 12), (3, 9), (4, 8)],
-    2: [(3, 10), (5, 6), (5, 7), (5, 8)],
-    3: [(2, 11), (2, 12), (4, 9)],
-}
-AT_END = [
-    (4, 10), (3, 11), (3, 12), (5, 9), (5, 10), (4, 11), (4, 12), (5, 11), (5, 12),
-]
+AT_BACK_HEAD = {0: [(0, 8)], 1: [(2, 0), (2, 1), (1, 4), (1, 5)], 2: [(1, 6), (1, 7), (2, 2), (2, 3)], 3: [(3, 0), (3, 1)], 4: [(1, 8), (0, 9)], 5: [(4, 0), (2, 4), (2, 5)], 6: [(4, 1), (1, 9)], 7: [(2, 6), (2, 7)], 8: [(3, 2), (3, 3), (3, 4), (0, 10)], 9: [(5, 0), (2, 8)], 10: [(5, 1), (4, 2), (3, 5), (2, 9), (1, 10)], 11: [(5, 2), (4, 3), (3, 6), (3, 7), (3, 8)]}
+AT_GRAD = {0: [(4, 4), (4, 5), (3, 9), (0, 11), (0, 12)], 1: [(4, 6)], 2: [(5, 3), (2, 10), (5, 4), (4, 7), (1, 11), (1, 12)], 3: [(5, 5), (5, 6)]}
+AT_END_A = [(5, 7), (4, 8), (3, 10), (4, 9), (2, 11), (2, 12), (5, 8), (5, 9), (4, 10), (3, 12), (3, 11)]
+AT_END_B = [(5, 10), (4, 12), (4, 11), (5, 12), (5, 11)]
 
 
 def bwd_kernel(heads, remote, *refs):
@@ -767,11 +777,11 @@
         vsum[...] = vgrad_ref[...]
     for i in range(n_tiles):
         if remote:
-            if i:
-                vector_wait()
             pump(AT_GRAD.get(i, ()))
-            if i < len(vector_steps):
-                vector_wait = vector_stage(*vector_steps[i])
+            if i != 2:
+                if i:
+                    vector_wait()
+                vector_wait = vector_stage(*vector_steps[min(i, 2)])
         prod = mm(rows2(w_in[0]), dproj[: 3 * gw, i * tm : (i + 1) * tm], NN)
         for g in range(1, groups):
             prod = prod + mm(rows2(w_in[g]), dproj[g * 3 * gw : (g + 1) * 3 * gw, i * tm : (i + 1) * tm], NN)
@@ -783,10 +793,10 @@
         if i + 2 < n_tiles:
             dfis[i + 2].start()
     if remote:
-        for i in range(n_tiles, len(vector_steps)):
-            vector_wait()
-            vector_wait = vector_stage(*vector_steps[i])
-        pump(AT_END)
+        pump(AT_END_A)
+        vector_wait()
+        vector_wait = vector_stage(*vector_steps[3])
+        pump(AT_END_B)
         vector_wait()
         vgrad_ref[...] = vsum[...]
         for unit in units:
@@ -863,6 +873,8 @@
     groups = heads // HG
     remote = n_shard == 8 and lax.axis_size("rep") == 4
 
+    q_order, k_order = [jnp.transpose(order, (1, 0, 2)) for order in (query_perm, key_perm)]
+
     def whole(rows):
         return lax.all_gather(rows, "shard", axis=0, tiled=True)
 
@@ -874,12 +886,9 @@
 
     weights = (in_weight, out_weight, inner_weight, outer_weight)
     short = jnp.stack([query_bias, value_bias, out_bias, first_gain, first_shift, outer_bias, second_gain, second_shift])
-    inner_piece = ff // n_shard
     if remote:
         w_in, w_out, w_inner, w_outer = [halved(w) for w in weights]
-        vec = lax.dynamic_update_slice(jnp.zeros((16, width), BF16), short, (0, shard * piece))
-        first = shard * inner_piece
-        vec = lax.dynamic_update_slice(vec, inner_bias[None], (8 + first // width, first % width))
+        vec = jnp.concatenate([short, inner_bias.reshape(-1, piece)])
     else:
         w_in, w_out, w_inner, w_outer = [whole(w) for w in weights]
         w_in = jnp.transpose(w_in.reshape(width, 3, groups, -1), (2, 0, 1, 3)).reshape(groups, 8, 2, width // 16, -1)
@@ -893,12 +902,12 @@
             ]
         )
     hidden, act, din, flow, dou, dfi, dbr, att, head, xt, vg, *wholes = fwd_call(
-        remote, layer_input[0], w_in, w_out, w_inner, w_outer, vec, segment_ids, token_valid, query_perm[0], key_perm[0], out_cotangent[0]
+        remote, layer_input[0], w_in, w_out, w_inner, w_outer, vec, segment_ids, token_valid, q_order, k_order, out_cotangent[0]
     )
     if remote:
         w_in, w_out = wholes
     grad_x, vg, g_outer, g_inner, g_out, g_in = bwd_call(
-        remote, act, din, flow, dou, dfi, dbr, att, head, xt, w_in, w_out, query_perm[0], key_perm[0], vg
+        remote, act, din, flow, dou, dfi, dbr, att, head, xt, w_in, w_out, q_order, k_order, vg
     )
     if not remote:
         g_in = jnp.transpose(g_in.reshape(groups, width, 3, -1), (1, 2, 0, 3))
@@ -914,6 +923,7 @@
         d_in, d_out, d_inner, d_outer = [summed(g) for g in grads]
         vg = lax.psum(vg, ("rep", "shard"))
     mine = lax.dynamic_slice(vg, (0, shard * piece), (8, piece))
+    inner_piece = ff // n_shard
     inner_mine = lax.dynamic_slice(vg[8 : 8 + ff // width].reshape(ff), (shard * inner_piece,), (inner_piece,))
     return (
         hidden[None], grad_x[None], d_in, mine[0], mine[1], d_out, mine[2], mine[3], mine[4], d_inner, inner_mine, d_outer,

time: 253 us -> 241 us (0.953)
  Pallas kernels: 233 us -> 222 us
    pallas_call x1, Pallas kernels: 124 us -> 117 us  [fwd_call(): pl.pallas_call(partial(fwd_kernel, heads, remote), out_shape=[jax.ShapeDt...]
    pallas_call x1, Pallas kernels: 109 us -> 105 us  [bwd_call(): pl.pallas_call(partial(bwd_kernel, heads, remote), out_shape=[jax.ShapeDt...]
where the time goes in v4:
time: 241 us; the launch traced here: 238 us
  Pallas kernels  222 us (92%)
  local copies, waits for them, and re-layouts  8.57 us (4%)
  other arithmetic  6 us (2%)
    pallas_call x1, Pallas kernels, fwd_call(): pl.pallas_call(partial(fwd_kernel, heads, remote), out_shape=[jax.ShapeDt...  117 us
    pallas_call x1, Pallas kernels, bwd_call(): pl.pallas_call(partial(bwd_kernel, heads, remote), out_shape=[jax.ShapeDt...  105 us
    convert_element_type x4, other arithmetic, shards(): d_in, d_out, d_inner, d_outer = [g.astype(F32) for g in grads]  6 us

profile of v4, /device:TPU:0, one launch (start us, length us, event | category | flops | bytes accessed | tf_op | source)
XLA Modules:
  0.0 237.9 jit_solution(14696647104008340602)
XLA Ops:
  0.6 0.8 reshape.64
  1.4 2.0 concatenate.3.refs_5_
  3.4 117.1 %layer_forward.1 = (bf16[1024,768]{1,0:T(8,128)(2,1)}, bf16[1024,3072]{1,0:T(8,128)(2,1)}, bf16[1024,3072]{1,0:T(8,128)(2,1)}, bf16[1024,768]{1,0:T(8,128)(2,1)}...) custom-call(bf16[1024,768]{1,0:T(8,128)(2,1)} %bitcast.48, ...), custom_call_target="tpu_custom_call" | custom-call | tf_op jit(solution)/shard_map/layer_forward/pallas_call | solution.py:581
  120.5 105.1 %layer_backward.1 = (bf16[1024,768]{1,0:T(8,128)(2,1)}, f32[16,768]{1,0:T(8,128)}, bf16[2,192,768]{2,1,0:T(8,128)(2,1)}, bf16[2,48,3072]{2,1,0:T(8,128)(2,1)}, b...) custom-call(bf16[1024,3072]{1,0:T(8,128)(2,1)} %get-tuple-element.35.refs_0_, ...), custom_call_target="tpu_custom_call" | custom-call | tf_op jit(solution)/shard_map/layer_backward/pallas_call | solution.py:851
  225.6 0.0 copy-start.3
  225.6 0.0 copy-start.2
  225.6 2.1 bitcast_convert_fusion.2
  227.7 0.8 constant_dynamic-slice_fusion
  228.5 0.5 slice_bitcast_fusion
  229.0 1.6 bitcast_convert_fusion.3
  230.7 0.0 copy-done.3
  230.7 0.0 copy-start
  230.7 1.2 bitcast_convert_fusion.1
  231.8 0.7 slice.32
  232.6 0.7 dynamic_slice.7
  233.2 0.0 copy-done.2
  233.2 1.1 bitcast_convert_fusion
  234.4 0.0 copy-done
  234.4 0.0 copy-start.1
  234.4 1.1 copy.36
  235.5 0.8 copy-done.1
  236.3 1.1 copy.37
  (1 shorter events, 0.0 us)
Async XLA Ops:
  225.6 5.1 %copy-start.3 = (bf16[2,48,3072]{2,1,0:T(8,128)(2,1)S(1)}, bf16[2,48,3072]{2,1,0:T(8,128)(2,1)}, u32[]{:S(2)}) copy-start(bf16[2,48,3072]{2,1,0:T(8,128)(2,1)} %get-tuple-element.51) | copy-start | bytes 1769476
  225.6 7.6 %copy-start.2 = (bf16[2,192,768]{2,1,0:T(8,128)(2,1)S(1)}, bf16[2,192,768]{2,1,0:T(8,128)(2,1)}, u32[]{:S(2)}) copy-start(bf16[2,192,768]{2,1,0:T(8,128)(2,1)} %get-tuple-element.52) | copy-start | bytes 1769476
  230.7 3.7 %copy-start = (bf16[1024,768]{1,0:T(8,128)(2,1)S(1)}, bf16[1024,768]{1,0:T(8,128)(2,1)}, u32[]{:S(2)}) copy-start(bf16[1024,768]{1,0:T(8,128)(2,1)} %get-tuple-element.34) | copy-start | bytes 4718596
  234.4 2.0 copy-start.1

commit v5 on v4

--- a/solution.py
+++ b/solution.py
@@ -246,9 +246,9 @@
 AT_START = [(1, 0), (1, 1), (1, 2)]
 AHEAD_A = [(2, 0), (1, 3), (2, 1), (1, 4), (2, 2), (1, 5), (3, 0), (3, 1), (2, 3), (1, 6), (3, 2), (2, 4), (1, 7)]
 AHEAD_B = [(4, 0), (4, 1), (5, 0), (5, 1)]
-AT_HEAD = {0: [(3, 3), (2, 5), (1, 8)], 1: [(4, 2), (2, 6), (3, 4), (2, 7), (1, 9), (1, 10)], 2: [(3, 5)], 3: [(4, 3), (2, 8), (1, 11)], 4: [(4, 4), (3, 6), (2, 9), (1, 12), (5, 2)], 5: [(3, 7), (2, 10), (2, 11)], 6: [(4, 5)], 7: [(4, 6), (3, 8), (2, 12)], 8: [(3, 9), (5, 3)], 11: [(4, 7), (4, 8)]}
-AT_FFN = [(3, 10), (3, 11), (5, 4), (5, 5), (5, 6), (5, 7), (5, 8)]
-AT_TILE = {1: [(4, 9), (3, 12)], 2: [(4, 10), (4, 11)], 3: [(4, 12)]}
+AT_HEAD = {0: [(3, 3), (2, 5), (1, 8)], 1: [(4, 2), (2, 6), (1, 9), (3, 4)], 2: [(2, 7), (3, 5), (1, 10)], 3: [(4, 3), (2, 8), (1, 11)], 4: [(3, 6), (2, 9), (4, 4), (1, 12), (5, 2)], 5: [(3, 7), (2, 10)], 6: [(4, 5), (2, 11)], 7: [(4, 6), (3, 8), (2, 12)], 8: [(5, 3)], 9: [(3, 9)], 11: [(4, 7), (4, 8)]}
+AT_FFN = [(5, 4), (5, 5), (5, 6), (5, 7), (5, 8)]
+AT_TILE = {0: [(3, 10), (3, 11)], 1: [(4, 9), (3, 12)], 2: [(4, 10)], 3: [(4, 11), (4, 12)]}
 AT_BACK = [(5, 9), (5, 10), (5, 11), (5, 12)]
 STAGES = ("", "first", "second", "third", "fourth", "last")
 

time: 241 us -> 241 us (level)
  no operation moved by 1% of the time
where the time goes in v5:
time: 241 us; the launch traced here: 237 us
  Pallas kernels  222 us (92%)
  local copies, waits for them, and re-layouts  8.57 us (4%)
  other arithmetic  6 us (2%)
    pallas_call x1, Pallas kernels, fwd_call(): pl.pallas_call(partial(fwd_kernel, heads, remote), out_shape=[jax.ShapeDt...  116 us
    pallas_call x1, Pallas kernels, bwd_call(): pl.pallas_call(partial(bwd_kernel, heads, remote), out_shape=[jax.ShapeDt...  106 us
    convert_element_type x4, other arithmetic, shards(): d_in, d_out, d_inner, d_outer = [g.astype(F32) for g in grads]  6 us

profile of v5, /device:TPU:0, one launch (start us, length us, event | category | flops | bytes accessed | tf_op | source)
XLA Modules:
  0.0 237.4 jit_solution(10116086917895095798)
XLA Ops:
  0.6 0.8 reshape.64
  1.4 2.0 concatenate.3.refs_5_
  3.4 116.2 %layer_forward.1 = (bf16[1024,768]{1,0:T(8,128)(2,1)}, bf16[1024,3072]{1,0:T(8,128)(2,1)}, bf16[1024,3072]{1,0:T(8,128)(2,1)}, bf16[1024,768]{1,0:T(8,128)(2,1)}...) custom-call(bf16[1024,768]{1,0:T(8,128)(2,1)} %bitcast.48, ...), custom_call_target="tpu_custom_call" | custom-call | tf_op jit(solution)/shard_map/layer_forward/pallas_call | solution.py:581
  119.5 105.6 %layer_backward.1 = (bf16[1024,768]{1,0:T(8,128)(2,1)}, f32[16,768]{1,0:T(8,128)}, bf16[2,192,768]{2,1,0:T(8,128)(2,1)}, bf16[2,48,3072]{2,1,0:T(8,128)(2,1)}, b...) custom-call(bf16[1024,3072]{1,0:T(8,128)(2,1)} %get-tuple-element.35.refs_0_, ...), custom_call_target="tpu_custom_call" | custom-call | tf_op jit(solution)/shard_map/layer_backward/pallas_call | solution.py:851
  225.1 0.0 copy-start.3
  225.1 0.0 copy-start.2
  225.1 2.1 bitcast_convert_fusion.2
  227.2 0.8 constant_dynamic-slice_fusion
  228.0 0.5 slice_bitcast_fusion
  228.5 1.6 bitcast_convert_fusion.3
  230.2 0.0 copy-done.3
  230.2 0.0 copy-start
  230.2 1.2 bitcast_convert_fusion.1
  231.3 0.7 slice.32
  232.1 0.7 dynamic_slice.7
  232.7 0.0 copy-done.2
  232.7 1.1 bitcast_convert_fusion
  233.8 0.0 copy-done
  233.9 0.0 copy-start.1
  233.9 1.1 copy.36
  235.0 0.8 copy-done.1
  235.8 1.1 copy.37
  (1 shorter events, 0.0 us)
Async XLA Ops:
  225.1 5.1 %copy-start.3 = (bf16[2,48,3072]{2,1,0:T(8,128)(2,1)S(1)}, bf16[2,48,3072]{2,1,0:T(8,128)(2,1)}, u32[]{:S(2)}) copy-start(bf16[2,48,3072]{2,1,0:T(8,128)(2,1)} %get-tuple-element.51) | copy-start | bytes 1769476
  225.1 7.6 %copy-start.2 = (bf16[2,192,768]{2,1,0:T(8,128)(2,1)S(1)}, bf16[2,192,768]{2,1,0:T(8,128)(2,1)}, u32[]{:S(2)}) copy-start(bf16[2,192,768]{2,1,0:T(8,128)(2,1)} %get-tuple-element.52) | copy-start | bytes 1769476
  230.2 3.7 %copy-start = (bf16[1024,768]{1,0:T(8,128)(2,1)S(1)}, bf16[1024,768]{1,0:T(8,128)(2,1)}, u32[]{:S(2)}) copy-start(bf16[1024,768]{1,0:T(8,128)(2,1)} %get-tuple-element.34) | copy-start | bytes 4718596
  233.9 2.0 copy-start.1
